TPU v7x, 512 devices: a whole 4x8x8 slice. The times are simulated.
512 devices in a mesh: mem: 8 (over x, core), par: 64 (over y, z).
Axes of the slice: x: 4, y: 8, z: 8, core: 2. Of those that a mesh axis runs over, the one named last changes fastest.
Arguments:
- operator: float32 [131072, 512], P('par'), may hold values from -0.046875 to 0.046875
- ensemble: float32 [256, 131072], P('mem', 'par'), may hold values from -6 to 6
- noise: float32 [256, 512], P('mem'), may hold values from -6 to 6
- observations: float32 [16384], replicated, may hold values from -6 to 6
- variances: float32 [16384], replicated, may hold values from 0.25 to 4
- rows: int32 [512], replicated, may hold values from 0 to 16383
Outputs:
- updated: float32 [256, 131072], P('mem', 'par')
Inputs may be any that keep to these rules, and one draw needn't show every extreme that they name: `rows`: indices into the observations; they may repeat.
All inputs are finite; a program needn't handle non-finite values.
Results may differ from a plain program's by a relative error of at most 0.00017.
Values sent between devices are 32-bit elements; how exact they have to be, the bound alone decides.
A program may use at most 64 MiB of HBM per device.

v0:
```python
import jax
import jax.numpy as jnp
from jax import lax
from jax.sharding import PartitionSpec as P


def cut_along(shard, dim, length):
    shape = shard.shape
    parts = shard.reshape(*shape[:dim], length, shape[dim] // length, *shape[dim + 1 :])
    return jnp.moveaxis(parts, dim, 0)


def sum_at_owner(shard, axis, dim):
    length = lax.axis_size(axis)
    parts = lax.all_to_all(cut_along(shard, dim, length), axis, 0, 0, tiled=True)
    return jnp.sum(parts, axis=0)


def padded_to(lines, length):
    spare = -lines.shape[0] % length
    if not spare:
        return lines
    return jnp.concatenate([lines, jnp.zeros((spare, *lines.shape[1:]), lines.dtype)])


def joined_along(parts, dim):
    parts = jnp.moveaxis(parts, 0, dim)
    shape = parts.shape
    return parts.reshape(*shape[:dim], shape[dim] * shape[dim + 1], *shape[dim + 2 :])


def from_everyone(shard, axis):
    copies = jnp.broadcast_to(shard, (lax.axis_size(axis), *shard.shape))
    return lax.all_to_all(copies, axis, split_axis=0, concat_axis=0, tiled=True)


def collect(shard, axis, dim):
    return joined_along(from_everyone(shard, axis), dim)


def total_of(shard, axes):
    lines = shard.reshape(-1)
    own = sum_at_owner(padded_to(lines, lax.axis_size(axes)), axes, 0)
    whole = collect(own, axes, 0)
    return whole[: len(lines)].reshape(shard.shape)


def sent_together(arrays, axis, dim, along):
    both = jnp.concatenate(arrays, axis=along)
    whole, at, outs = (lax.all_gather(both, axis, axis=dim, tiled=True), 0, [])
    for a in arrays:
        outs.append(lax.slice_in_dim(whole, at, at + a.shape[along], axis=along))
        at += a.shape[along]
    return tuple(outs)


def cholesky_solve(matrix, right):
    factor = jnp.linalg.cholesky(matrix)
    inner = lax.linalg.triangular_solve(factor, right, left_side=True, lower=True)
    return lax.linalg.triangular_solve(factor, inner, left_side=True, lower=True, transpose_a=True)


def per_device(operator, ensemble, noise, observations, variances, rows):
    highest = lax.Precision.HIGHEST
    own_members = ensemble.shape[0]
    member_index = lax.axis_index("mem")
    partial_fwd = jnp.dot(ensemble, operator, precision=highest, preferred_element_type=jnp.float32)
    forward = total_of(partial_fwd, "par")
    obs_rows = jnp.take(observations, rows)
    var_rows = jnp.take(variances, rows)
    residual = obs_rows[None, :] + jnp.sqrt(var_rows)[None, :] * noise - forward
    all_forward, all_residual = sent_together((forward, residual), "mem", 0, 1)
    spread = all_forward - jnp.mean(all_forward, axis=0, keepdims=True)
    weighted = spread / var_rows[None, :]
    gram_part = jnp.dot(weighted, spread.T, precision=highest, preferred_element_type=jnp.float32)
    cross_part = jnp.dot(
        weighted, all_residual.T, precision=highest, preferred_element_type=jnp.float32
    )
    members = all_forward.shape[0]
    gram = gram_part + (members - 1) * jnp.eye(members, dtype=jnp.float32)
    weights = cholesky_solve(gram, cross_part)
    gathered = collect(ensemble, "mem", 0)
    deviation = gathered - jnp.mean(gathered, axis=0, keepdims=True)
    own_columns = lax.dynamic_slice_in_dim(weights, member_index * own_members, own_members, 1)
    change = jnp.dot(
        own_columns.T, deviation, precision=highest, preferred_element_type=jnp.float32
    )
    return ensemble + change


def solution(mesh):
    return jax.shard_map(
        per_device,
        mesh=mesh,
        in_specs=(P("par", None), P("mem", "par"), P("mem", None), P(), P(), P()),
        out_specs=P("mem", "par"),
        check_vma=False,
    )
```

profile of v0, /device:TPU:1, one launch (start us, length us, event | category | flops | bytes accessed | tf_op | source)
XLA Modules:
  0.0 170.2 jit_solution(2197274596058909621)
XLA Ops:
  6.5 4.8 %fusion.27 = f32[32,512]{1,0:T(8,128)S(1)} fusion(f32[32,2048]{1,0:T(8,128)} %param.9, f32[2048,512]{1,0:T(8,128)} %param.8), kind=kOutput, calls=%fused_computation.65 | convolution fusion | flops 402653184 | bytes 4521984 | tf_op jit(solution)/shard_map/dot_general | solution.py:67
  11.4 28.1 %all_to_all.21 = f32[64,1,256]{2,1,0:T(1,128)S(1)} all-to-all(f32[64,1,256]{2,1,0:T(1,128)S(1)} %all_to_all.17), channel_id=1, replica_groups=mesh['mem'=8,'par'=64] {'par'}, dimensions={0} | all-to-all | bytes 131072 | tf_op jit(solution)/shard_map/all_to_all | solution.py:15
  39.6 14.9 %all_to_all.22 = f32[64,1,256]{2,1,0:T(1,128)S(1)} all-to-all(f32[64,1,256]{2,1,0:T(1,128)S(1)} %broadcast_in_dim.12), channel_id=1, replica_groups=mesh['mem'=8,'par'=64] {'par'}, dimensions={0} | all-to-all | bytes 131072 | tf_op jit(solution)/shard_map/all_to_all | solution.py:34
  54.5 1.6 broadcast_in_dim.20
  56.1 7.7 %all-to-all-start.2 = ((f32[8,32,2048]{2,1,0:T(8,128)}), f32[8,32,2048]{2,1,0:T(8,128)S(1)}, u32[]{:S(2)}, u32[]{:S(2)}) async-start(f32[8,32,2048]{2,1,0:T(8,128)} %broadcast_in_dim.20), calls=%async_computation.2 | async-start | bytes 4194304 | tf_op jit(solution)/shard_map/all_to_all | solution.py:34
  63.8 3.1 %gather_fusion.1 = f32[512]{0:T(512)S(1)} fusion(f32[16384]{0:T(1024)S(1)} %copy-done, s32[1024]{0:T(1024)S(1)} %pad_clamp_fusion), kind=kCustom, calls=%fused_computation.1.clone | custom fusion | bytes 6144 | tf_op jit(solution)/shard_map/jit(_take)/gather | solution.py:70
  67.0 3.3 %gather_fusion = f32[512]{0:T(512)S(1)} fusion(f32[16384]{0:T(1024)S(1)} %copy-done.1, s32[1024]{0:T(1024)S(1)} %pad_clamp_fusion), kind=kCustom, calls=%fused_computation.clone | custom fusion | bytes 6144 | tf_op jit(solution)/shard_map/jit(_take)/gather | solution.py:69
  70.6 0.7 pad_maximum_fusion
  71.3 22.9 %all-to-all-done.2 = f32[8,32,2048]{2,1,0:T(8,128)S(1)} async-done(((f32[8,32,2048]{2,1,0:T(8,128)}), f32[8,32,2048]{2,1,0:T(8,128)S(1)}, u32[]{:S(2)}, u32[]{:S(2)}) %all-to-all-start.2) | async-done | bytes 2097184 | tf_op jit(solution)/shard_map/all_to_all | solution.py:34
  94.3 1.6 bitcast_subtract_fusion
  95.9 1.1 slice_reduce_fusion
  97.0 1.9 %fusion.3 = f32[256,256]{1,0:T(8,128)S(1)} fusion(f32[256,1024]{1,0:T(8,128)} %all-gather.2.cloned.1.call-done, f32[512]{0:T(512)S(1)} %get-tuple-element.23, f32[512]{0:T(512)S(1)} %broadcast_multiply_fusion.1), kind=kOutput, calls=%fused_computation.14 | convolution fusion | flops 403046400 | bytes 1316864 | tf_op jit(solution)/shard_map/dot_general | solution.py:75
  99.2 11.7 %cholesky.49 = f32[128,128]{1,0:T(8,128)S(1)} custom-call(f32[128,128]{1,0:T(8,128)S(1)} %cholesky.115), custom_call_target="Cholesky" | custom-call | tf_op jit(solution)/shard_map/jit(cholesky)/cholesky | solution.py:58
  110.9 9.8 %custom-call.16 = f32[1,128,128]{1,2,0:T(8,128)S(1)} custom-call(f32[1,128,128]{2,1,0:T(8,128)S(1)} %get-tuple-element.29), custom_call_target="InvertDiagBlocksLowerTriangular" | custom-call | tf_op jit(solution)/shard_map/jit(cholesky)/cholesky | solution.py:58
  120.8 0.2 constant_dynamic-update-slice_fusion
  121.0 0.3 convolution_subtract_fusion.2
  121.2 11.7 %cholesky.103 = f32[128,128]{1,0:T(8,128)S(1)} custom-call(f32[128,128]{1,0:T(8,128)S(1)} %convolution_subtract_fusion.2), custom_call_target="Cholesky" | custom-call | tf_op jit(solution)/shard_map/jit(cholesky)/cholesky | solution.py:58
  133.0 0.7 compare_reduce_fusion
  135.0 3.9 %while.1 = (s32[]{:T(128)}, f32[256,256]{1,0:T(8,128)S(1)}, s32[2,2]{1,0:T(2,128)S(1)}, f32[2,128,128]{2,1,0:T(8,128)S(1)}, s32[]{:T(128)}) while((s32[]{:T(128)}, f32[256,256]{1,0:T(8,128)S(1)}, s32[2,2]{1,0:T(2,128)S(1)}, f32[2,128,128]{2,1,0:T(8,128)S(1)}, s32[]{:T(128)}) %tuple.26), condition=%wide.while_cond, body=%wide.while_body.sunk | while | flops 2 | bytes 131189 | solution.py:60
  135.0 0.6 fusion.39
  135.6 1.4 bitcast_dynamic-update-slice_fusion.2
  137.0 0.6 fusion.39
  137.6 1.4 bitcast_dynamic-update-slice_fusion.2
  139.0 19.9 %custom-call.17 = f32[2,128,128]{1,2,0:T(8,128)S(1)} custom-call(f32[2,128,128]{2,1,0:T(8,128)S(1)} %get-tuple-element.13), custom_call_target="InvertDiagBlocksLowerTriangular" | custom-call | tf_op jit(solution)/shard_map/triangular_solve | solution.py:60
  158.9 0.6 fusion
  159.5 0.3 fusion.13
  159.8 0.3 convolution_subtract_fusion.1
  160.1 0.3 fusion.20
  160.4 0.3 fusion.19
  160.7 0.3 convolution_subtract_fusion
  161.0 0.3 fusion.18
  161.3 2.1 %convolution_add_fusion = f32[32,2048]{1,0:T(8,128)} fusion(f32[32,2048]{1,0:T(8,128)S(1)} %copy-done.3, f32[256,2048]{1,0:T(8,128)S(1)} %copy-done.2, s32[]{:T(128)S(6)} %select_n.15, f32[128,256]{1,0:T(8,128)S(1)} %fusion.18, f32[128,256]{1,0:T(8,128)S(1)} %fusion.19), kind=kOutput, calls=%fused_computation.4 | convolution fusion | flops 201400320 | bytes 2883588 | tf_op jit(solution)/shard_map/dot_general | solution.py:85
  (41 shorter events, 1.0 us)
Async XLA Ops:
  6.5 57.3 %copy-start = (f32[16384]{0:T(1024)S(1)}, f32[16384]{0:T(1024)}, u32[]{:S(2)}) copy-start(f32[16384]{0:T(1024)} %param.12) | copy-start | bytes 196612
  6.5 48.0 %copy-start.3 = (f32[32,2048]{1,0:T(8,128)S(1)}, f32[32,2048]{1,0:T(8,128)}, u32[]{:S(2)}) copy-start(f32[32,2048]{1,0:T(8,128)} %param.9) | copy-start | bytes 786436
  56.1 7.7 %copy-start.6 = (s32[512]{0:T(512)S(1)}, s32[512]{0:T(512)}, u32[]{:S(2)}) copy-start(s32[512]{0:T(512)} %param.13) | copy-start | bytes 6148
  56.1 38.1 %all-to-all-start.2 = ((f32[8,32,2048]{2,1,0:T(8,128)}), f32[8,32,2048]{2,1,0:T(8,128)S(1)}, u32[]{:S(2)}, u32[]{:S(2)}) async-start(f32[8,32,2048]{2,1,0:T(8,128)} %broadcast_in_dim.20), calls=%async_computation.2 | async-start | bytes 4194304 | tf_op jit(solution)/shard_map/all_to_all | solution.py:34
  63.8 3.2 %copy-start.1 = (f32[16384]{0:T(1024)S(1)}, f32[16384]{0:T(1024)}, u32[]{:S(2)}) copy-start(f32[16384]{0:T(1024)} %param.11) | copy-start | bytes 196612
  63.8 32.1 %all-gather.2.cloned.1.call-start = ((), (), s32[]{:S(2)}) async-start(), calls=%async_computation.3 | async-start | bytes 1179648 | tf_op jit(solution)/shard_map/all_gather | solution.py:50
  63.8 6.7 %copy-start.5 = (f32[32,512]{1,0:T(8,128)S(1)}, f32[32,512]{1,0:T(8,128)}, u32[]{:S(2)}) copy-start(f32[32,512]{1,0:T(8,128)} %param.10) | copy-start | bytes 196612
  98.9 59.9 %copy-start.4 = (f32[256,1024]{1,0:T(8,128)S(1)}, f32[256,1024]{1,0:T(8,128)}, u32[]{:S(2)}) copy-start(f32[256,1024]{1,0:T(8,128)} %all-gather.2.cloned.1.call-done) | copy-start | bytes 3145732
  158.9 2.4 %copy-start.2 = (f32[256,2048]{1,0:T(8,128)S(1)}, f32[256,2048]{1,0:T(8,128)}, u32[]{:S(2)}) copy-start(f32[256,2048]{1,0:T(8,128)} %bitcast_subtract_fusion) | copy-start | bytes 6291460
Sparse Core Ops, SparseCore 0:
  71.4 22.3 all-gather.1
where the time goes:
time: 171 us; the launch traced here: 170 us
  other arithmetic  57.7 us (34%)
  blocking collectives  42.9 us (25%)
  waiting for transfers between devices  22.9 us (13%)
  between operations  15 us (9%)
  local copies, waits for them, and re-layouts  12.3 us (7%)
  matrix products  11.6 us (7%)
  starting transfers between devices  7.69 us (4%)
    another operation x6, other arithmetic, cholesky_solve(): factor = jnp.linalg.cholesky(matrix)  34 us
    all_to_all x1, blocking collectives, sum_at_owner(): lax.all_to_all(cut_along(shard, dim, length), axis, 0, 0, tiled=True)  28.1 us
    all_to_all x1, waiting for transfers between devices, from_everyone(): return lax.all_to_all(copies, axis, split_axis=0, concat_axis=0, tiled=True)  22.9 us
    another operation x3, other arithmetic, cholesky_solve(): lax.linalg.triangular_solve(factor, inner, left_side=True, lower=True, tr...  19.9 us
    all_to_all x1, blocking collectives, from_everyone(): return lax.all_to_all(copies, axis, split_axis=0, concat_axis=0, tiled=True)  14.9 us
    all_to_all x1, starting transfers between devices, from_everyone(): return lax.all_to_all(copies, axis, split_axis=0, concat_axis=0, tiled=True)  7.69 us
    dot_general x1, matrix products, per_device(): jnp.dot(ensemble, operator, precision=highest, preferred_element_type=jnp...  4.78 us
    another operation x6, local copies, waits for them, and re-layouts  3.9 us
  transfers between devices with their start and end apart: 2, of which 1 were waited for; matrix products, arithmetic and copies ran while one was open for 5% of the time, Pallas kernels for 0%

commit v1 on v0

v1 whole, which is shorter than its diff:
```python
import functools

import jax
import jax.numpy as jnp
from jax import lax
from jax.experimental import pallas as pl
from jax.experimental.pallas import tpu as pltpu
from jax.sharding import PartitionSpec as P

MESH = pl.DeviceIdType.MESH
CHUNKS = 8
F32 = jnp.float32
BF16 = jnp.bfloat16


def split(a):
    hi = a.astype(BF16)
    return hi, (a - hi.astype(F32)).astype(BF16)


def dot(a, b):
    return jnp.dot(a, b, preferred_element_type=F32)


def exchange_kernel(
    op_hbm, ens_hbm, fwd_all, ens_all,
    op_v, ens_v, zsrc, zrecv, ysrc, yrecv, fz,
    op_sem, ens_sem, own_sem,
    zs_sem, zr_sem, ys_sem, yr_sem, gs_sem, gr_sem,
    xs_sem, xr_sem, cs_sem, cr_sem,
    es_sem, er_sem, fs_sem, fr_sem,
):
    mem = lax.axis_index("mem")
    par = lax.axis_index("par")
    x, core = mem // 2, mem % 2
    y, z = par // 8, par % 8
    own = ens_hbm.shape[0]
    depth = op_hbm.shape[0] // CHUNKS
    twin = x * 2 + (1 - core)

    def at_z(d):
        return (mem, y * 8 + (z + d) % 8)

    def at_y(d):
        return (mem, ((y + d) % 8) * 8 + z)

    def mem_at(d):
        return ((x + d) % 4) * 2 + core

    ens_copy = pltpu.make_async_copy(ens_hbm, ens_v, ens_sem)
    ens_copy.start()
    op_copies = []
    for c in range(CHUNKS):
        rows = pl.ds(c * depth, depth)
        op_copies.append(pltpu.make_async_copy(op_hbm.at[rows], op_v.at[rows], op_sem.at[c]))
        op_copies[-1].start()

    barrier = pltpu.get_barrier_semaphore()
    friends = [at_z(d) for d in range(1, 8)] + [at_y(d) for d in range(1, 8)]
    friends += [(mem_at(d), par) for d in range(1, 4)] + [(twin, par)]
    for friend in friends:
        pl.semaphore_signal(barrier, inc=1, device_id=friend, device_id_type=MESH)
    pl.semaphore_wait(barrier, len(friends))

    def remote(src, dst, send, recv, device):
        copy = pltpu.make_async_remote_copy(
            src_ref=src, dst_ref=dst, send_sem=send, recv_sem=recv, device_id=device, device_id_type=MESH
        )
        copy.start()
        return copy

    own_rows = pl.ds(pl.multiple_of(mem * own, own), own)
    ens_out = [
        remote(ens_hbm, ens_all.at[own_rows], es_sem.at[d], er_sem.at[d], (mem_at(d), par)) for d in range(1, 4)
    ]
    twin_out = [remote(ens_hbm, ens_all.at[own_rows], fs_sem.at[0], fr_sem.at[0], (twin, par))]

    ens_copy.wait()
    own_copy = pltpu.make_async_copy(ens_v, ens_all.at[own_rows], own_sem)
    own_copy.start()

    total = jnp.zeros((own, op_hbm.shape[1]), F32)
    for c in range(CHUNKS):
        op_copies[c].wait()
        op_hi, op_lo = split(op_v[pl.ds(c * depth, depth), :])
        ens_hi, ens_lo = split(ens_v[:, pl.ds(c * depth, depth)])
        total += dot(ens_hi, op_hi) + dot(ens_lo, op_hi) + dot(ens_hi, op_lo)
    for q in range(8):
        zsrc[q] = total[(q // 4) * 16 : (q // 4) * 16 + 16, (q % 4) * 128 : (q % 4) * 128 + 128]

    z_out = [
        remote(zsrc.at[(z + d) % 8], zrecv.at[d], zs_sem.at[d], zr_sem.at[d], at_z(d)) for d in range(1, 8)
    ]
    part = zsrc[z]
    for d in range(1, 8):
        z_out[d - 1].wait_recv()
        part += zrecv[d]
    ysrc[...] = part
    y_out = [remote(ysrc, yrecv.at[d], ys_sem.at[d], yr_sem.at[d], at_y(d)) for d in range(1, 8)]
    for d in range(1, 8):
        y_out[d - 1].wait_recv()
        part += yrecv[d]
    fz[z] = part
    g_out = [remote(fz.at[z], fz.at[z], gs_sem.at[d], gr_sem.at[d], at_z(d)) for d in range(1, 8)]

    def forward_ens(d):
        ens_out[d - 1].wait_recv()
        rows = pl.ds(pl.multiple_of(((x + 4 - d) % 4) * 2 * own + core * own, own), own)
        twin_out.append(remote(ens_all.at[rows], ens_all.at[rows], fs_sem.at[d], fr_sem.at[d], (twin, par)))

    forward_ens(1)
    forward_ens(3)
    for d in range(1, 8):
        g_out[d - 1].wait_recv()
    x_out = [remote(fz, fwd_all.at[mem], xs_sem.at[d], xr_sem.at[d], (mem_at(d), par)) for d in range(1, 4)]
    c_out = [remote(fz, fwd_all.at[mem], cs_sem.at[0], cr_sem.at[0], (twin, par))]
    fwd_all[mem] = fz[...]
    forward_ens(2)
    for d in (1, 3, 2):
        x_out[d - 1].wait_recv()
        came = ((x + 4 - d) % 4) * 2 + core
        c_out.append(remote(fwd_all.at[came], fwd_all.at[came], cs_sem.at[d], cr_sem.at[d], (twin, par)))
    for copy in c_out + twin_out:
        copy.wait()
    for copy in z_out + y_out + g_out + ens_out + x_out:
        copy.wait_send()
    own_copy.wait()


def exchange(operator, ensemble):
    own, params = ensemble.shape
    rows = operator.shape[1]
    any_spec = pl.BlockSpec(memory_space=pl.ANY)
    dma = pltpu.SemaphoreType.DMA
    return pl.pallas_call(
        exchange_kernel,
        name="exchange",
        out_shape=(
            jax.ShapeDtypeStruct((8, 8, 16, 128), F32),
            jax.ShapeDtypeStruct((8 * own, params), F32),
        ),
        in_specs=[any_spec, any_spec],
        out_specs=(pl.BlockSpec(memory_space=pltpu.VMEM), any_spec),
        scratch_shapes=[
            pltpu.VMEM((params, rows), F32),
            pltpu.VMEM((own, params), F32),
            pltpu.VMEM((8, 16, 128), F32),
            pltpu.VMEM((8, 16, 128), F32),
            pltpu.VMEM((16, 128), F32),
            pltpu.VMEM((8, 16, 128), F32),
            pltpu.VMEM((8, 16, 128), F32),
            dma((CHUNKS,)), dma, dma,
            dma((8,)), dma((8,)), dma((8,)), dma((8,)), dma((8,)), dma((8,)),
            dma((4,)), dma((4,)), dma((4,)), dma((4,)),
            dma((4,)), dma((4,)), dma((4,)), dma((4,)),
        ],
        compiler_params=pltpu.CompilerParams(collective_id=0, has_side_effects=True),
    )(operator, ensemble)


def cholesky_solve(matrix, right):
    factor = jnp.linalg.cholesky(matrix)
    inner = lax.linalg.triangular_solve(factor, right, left_side=True, lower=True)
    return lax.linalg.triangular_solve(factor, inner, left_side=True, lower=True, transpose_a=True)


def per_device(operator, ensemble, noise, observations, variances, rows):
    highest = lax.Precision.HIGHEST
    own_members = ensemble.shape[0]
    member_index = lax.axis_index("mem")
    obs_rows = jnp.take(observations, rows)
    var_rows = jnp.take(variances, rows)
    pieces, gathered = exchange(operator, ensemble)
    all_forward = pieces.reshape(8, 2, 4, 16, 128).transpose(0, 1, 3, 2, 4).reshape(256, 512)
    forward = lax.dynamic_slice_in_dim(all_forward, member_index * own_members, own_members, 0)
    residual = obs_rows[None, :] + jnp.sqrt(var_rows)[None, :] * noise - forward
    spread = all_forward - jnp.mean(all_forward, axis=0, keepdims=True)
    weighted = spread / var_rows[None, :]
    gram_part = jnp.dot(weighted, spread.T, precision=highest, preferred_element_type=jnp.float32)
    cross_part = jnp.dot(weighted, residual.T, precision=highest, preferred_element_type=jnp.float32)
    members = all_forward.shape[0]
    gram = gram_part + (members - 1) * jnp.eye(members, dtype=jnp.float32)
    weights = cholesky_solve(gram, cross_part)
    deviation = gathered - jnp.mean(gathered, axis=0, keepdims=True)
    change = jnp.dot(weights.T, deviation, precision=highest, preferred_element_type=jnp.float32)
    return ensemble + change


def solution(mesh):
    return jax.shard_map(
        per_device,
        mesh=mesh,
        in_specs=(P("par", None), P("mem", "par"), P("mem", None), P(), P(), P()),
        out_specs=P("mem", "par"),
        check_vma=False,
    )
```

time: 171 us -> 115 us (0.67)
  blocking collectives: 42.9 us -> 0 us
  Pallas kernels: 0 us -> 39.2 us
  waiting for transfers between devices: 22.9 us -> 0 us
  between operations: 15 us -> 1.54 us
  starting transfers between devices: 7.69 us -> 0 us
  matrix products: 11.6 us -> 4.99 us
    all_to_all x2 -> x0, blocking collectives: 42.9 us -> none  [the longest x1 28.1 us: sum_at_owner(): lax.all_to_all(cut_along(shard, dim, length), axis, 0, 0, tiled=True)]
    pallas_call x0 -> x1, Pallas kernels: none -> 39.2 us  [exchange(): pl.pallas_call(exchange_kernel, name='exchange', out_shape=(jax.ShapeDtyp...]
    all_to_all x1 -> x0, waiting for transfers between devices: 22.9 us -> none  [from_everyone(): return lax.all_to_all(copies, axis, split_axis=0, concat_axis=0, tiled=True)]
    all_to_all x1 -> x0, starting transfers between devices: 7.69 us -> none  [from_everyone(): return lax.all_to_all(copies, axis, split_axis=0, concat_axis=0, tiled=True)]
    dot_general x3 -> x2, matrix products: 7.47 us -> 2.63 us  [the longest x1 2.06 us: per_device(): jnp.dot(weights.T, deviation, precision=highest, preferred_element_type=j...]
    another operation x7 -> x6, local copies, waits for them, and re-layouts: 3.92 us -> 3.83 us
  transfers between devices with their start and end apart: 2 -> 0, of which waited for: 1 -> 0; matrix products, arithmetic and copies ran while one was open for 5% -> 0% of each run, Pallas kernels for 0% -> 0%
where the time goes in v1:
time: 115 us; the launch traced here: 114 us
  other arithmetic  58 us (50%)
  Pallas kernels  39.2 us (34%)
  local copies, waits for them, and re-layouts  10.7 us (9%)
  matrix products  4.99 us (4%)
  between operations  1.54 us (1%)
    pallas_call x1, Pallas kernels, exchange(): pl.pallas_call(exchange_kernel, name='exchange', out_shape=(jax.ShapeDtyp...  39.2 us
    another operation x6, other arithmetic, cholesky_solve(): factor = jnp.linalg.cholesky(matrix)  34.1 us
    another operation x3, other arithmetic, cholesky_solve(): lax.linalg.triangular_solve(factor, inner, left_side=True, lower=True, tr...  19.7 us
    another operation x6, local copies, waits for them, and re-layouts  3.83 us
    gather x1, local copies, waits for them, and re-layouts, per_device(): var_rows = jnp.take(variances, rows)  3.14 us
    gather x1, local copies, waits for them, and re-layouts, per_device(): obs_rows = jnp.take(observations, rows)  3.13 us

profile of v1, /device:TPU:1, one launch (start us, length us, event | category | flops | bytes accessed | tf_op | source)
XLA Modules:
  0.0 114.4 jit_solution(17249864916750400582)
XLA Ops:
  0.0 0.1 triangular_solve.72
  0.1 0.7 compare_select_fusion
  0.8 0.1 copy-done
  0.8 3.1 %gather_fusion.1 = f32[512]{0:T(512)S(1)} fusion(f32[16384]{0:T(1024)S(1)} %copy-done, s32[1024]{0:T(1024)S(1)} %pad_clamp_fusion), kind=kCustom, calls=%fused_computation.1.clone | custom fusion | bytes 6144 | tf_op jit(solution)/shard_map/jit(_take)/gather | solution.py:171
  4.0 3.1 %gather_fusion = f32[512]{0:T(512)S(1)} fusion(f32[16384]{0:T(1024)S(1)} %copy-done.1, s32[1024]{0:T(1024)S(1)} %pad_clamp_fusion), kind=kCustom, calls=%fused_computation.clone | custom fusion | bytes 6144 | tf_op jit(solution)/shard_map/jit(_take)/gather | solution.py:172
  7.2 39.2 %exchange.1 = (f32[8,8,16,128]{3,2,1,0:T(8,128)}, f32[256,2048]{1,0:T(8,128)}) custom-call(f32[2048,512]{1,0:T(8,128)} %op_hbm.1, f32[32,2048]{1,0:T(8,128)} %ens_hbm.1), custom_call_target="tpu_custom_call" | custom-call | tf_op jit(solution)/shard_map/exchange/pallas_call | solution.py:135
  46.4 1.4 %bitcast_reduce_fusion = f32[4,128]{1,0:T(4,128)S(1)} fusion(f32[8,2,4,16,128]{4,3,2,1,0:T(8,128)} %bitcast.61), kind=kLoop, calls=%fused_computation.17 | loop fusion | flops 130560 | bytes 526336 | tf_op jit(solution)/shard_map/reduce_sum | solution.py:177
  47.8 1.7 %reduce_sum.19 = f32[2048]{0:T(1024)S(1)} reduce(f32[256,2048]{1,0:T(8,128)} %get-tuple-element.9, f32[]{:T(128)} %constant.101.clone.1), dimensions={0}, to_apply=%region_5.7 | reduce | flops 522240 | bytes 2105348 | tf_op jit(solution)/shard_map/reduce_sum | solution.py:184
  49.5 0.2 copy.9
  49.8 0.6 fusion.7
  50.4 0.3 broadcast_divide_fusion
  50.7 0.6 fusion.2
  51.3 0.1 copy.10
  51.5 11.7 %cholesky.49 = f32[128,128]{1,0:T(8,128)S(1)} custom-call(f32[128,128]{1,0:T(8,128)S(1)} %cholesky.115), custom_call_target="Cholesky" | custom-call | tf_op jit(solution)/shard_map/jit(cholesky)/cholesky | solution.py:162
  63.3 9.8 %custom-call.16 = f32[1,128,128]{1,2,0:T(8,128)S(1)} custom-call(f32[1,128,128]{2,1,0:T(8,128)S(1)} %get-tuple-element.35), custom_call_target="InvertDiagBlocksLowerTriangular" | custom-call | tf_op jit(solution)/shard_map/jit(cholesky)/cholesky | solution.py:162
  73.1 0.2 constant_dynamic-update-slice_fusion
  73.3 0.3 convolution_subtract_fusion
  73.6 11.8 %cholesky.103 = f32[128,128]{1,0:T(8,128)S(1)} custom-call(f32[128,128]{1,0:T(8,128)S(1)} %convolution_subtract_fusion), custom_call_target="Cholesky" | custom-call | tf_op jit(solution)/shard_map/jit(cholesky)/cholesky | solution.py:162
  85.5 0.7 compare_reduce_fusion
  87.4 3.9 %while.1 = (s32[]{:T(128)}, f32[256,256]{1,0:T(8,128)S(1)}, s32[2,2]{1,0:T(2,128)S(1)}, f32[2,128,128]{2,1,0:T(8,128)S(1)}, s32[]{:T(128)}) while((s32[]{:T(128)}, f32[256,256]{1,0:T(8,128)S(1)}, s32[2,2]{1,0:T(2,128)S(1)}, f32[2,128,128]{2,1,0:T(8,128)S(1)}, s32[]{:T(128)}) %tuple.28), condition=%wide.while_cond, body=%wide.while_body.sunk | while | flops 2 | bytes 131189 | solution.py:164
  87.5 0.6 fusion.44
  88.1 1.3 %bitcast_dynamic-update-slice_fusion.2 = f32[2,128,128]{2,1,0:T(8,128)S(1)} fusion(f32[2,128,128]{2,1,0:T(8,128)S(1)} %get-tuple-element.80, s32[]{:T(128)S(6)} %copy.32, f32[256,256]{1,0:T(8,128)S(1)} %get-tuple-element.83, s32[]{:T(128)} %bitcast.59, s32[]{:T(128)} %bitcast.60), kind=kLoop, calls=%fused_computation.2.clone.1 | loop fusion | bytes 131084 | tf_op jit(solution)/shard_map/triangular_solve
  89.4 0.6 fusion.44
  90.0 1.3 %bitcast_dynamic-update-slice_fusion.2 = f32[2,128,128]{2,1,0:T(8,128)S(1)} fusion(f32[2,128,128]{2,1,0:T(8,128)S(1)} %get-tuple-element.80, s32[]{:T(128)S(6)} %copy.32, f32[256,256]{1,0:T(8,128)S(1)} %get-tuple-element.83, s32[]{:T(128)} %bitcast.59, s32[]{:T(128)} %bitcast.60), kind=kLoop, calls=%fused_computation.2.clone.1 | loop fusion | bytes 131084 | tf_op jit(solution)/shard_map/triangular_solve
  91.3 19.7 %custom-call.17 = f32[2,128,128]{1,2,0:T(8,128)S(1)} custom-call(f32[2,128,128]{2,1,0:T(8,128)S(1)} %get-tuple-element.17), custom_call_target="InvertDiagBlocksLowerTriangular" | custom-call | tf_op jit(solution)/shard_map/triangular_solve | solution.py:164
  111.0 0.2 fusion.20
  111.2 0.2 convolution_subtract_fusion.2
  111.4 0.3 fusion.22
  111.7 0.2 fusion.21
  111.9 0.2 convolution_subtract_fusion.1
  112.1 0.2 fusion.19
  112.4 2.1 %convolution_add_fusion = f32[32,2048]{1,0:T(8,128)} fusion(f32[32,2048]{1,0:T(8,128)S(1)} %copy-done.4, f32[256,2048]{1,0:T(8,128)S(1)} %copy-done.2, f32[2048]{0:T(1024)S(1)} %broadcast_multiply_fusion, f32[128,32]{0,1:T(8,128)S(1)} %fusion.21, f32[128,32]{0,1:T(8,128)S(1)} %fusion.19), kind=kOutput, calls=%fused_computation.4 | convolution fusion | flops 201924608 | bytes 2662400 | tf_op jit(solution)/shard_map/dot_general | solution.py:185
  (28 shorter events, 0.3 us)
Async XLA Ops:
  0.0 0.8 copy-start
  0.0 4.0 %copy-start.1 = (f32[16384]{0:T(1024)S(1)}, f32[16384]{0:T(1024)}, u32[]{:S(2)}) copy-start(f32[16384]{0:T(1024)} %param.12) | copy-start | bytes 196612
  0.8 6.3 %copy-start.5 = (s32[512]{0:T(512)S(1)}, s32[512]{0:T(512)}, u32[]{:S(2)}) copy-start(s32[512]{0:T(512)} %param.13) | copy-start | bytes 6148
  46.4 3.2 %copy-start.3 = (f32[8,8,16,128]{3,2,1,0:T(8,128)S(1)}, f32[8,8,16,128]{3,2,1,0:T(8,128)}, u32[]{:S(2)}) copy-start(f32[8,8,16,128]{3,2,1,0:T(8,128)} %get-tuple-element.8) | copy-start | bytes 1572868
  47.8 2.0 %copy-start.6 = (f32[32,512]{1,0:T(8,128)S(1)}, f32[32,512]{1,0:T(8,128)}, u32[]{:S(2)}) copy-start(f32[32,512]{1,0:T(8,128)} %param.10) | copy-start | bytes 196612
  51.4 60.9 %copy-start.2 = (f32[256,2048]{1,0:T(8,128)S(1)}, f32[256,2048]{1,0:T(8,128)}, u32[]{:S(2)}) copy-start(f32[256,2048]{1,0:T(8,128)} %get-tuple-element.9) | copy-start | bytes 6291460
  51.4 60.9 %copy-start.4 = (f32[32,2048]{1,0:T(8,128)S(1)}, f32[32,2048]{1,0:T(8,128)}, u32[]{:S(2)}) copy-start(f32[32,2048]{1,0:T(8,128)} %ens_hbm.1) | copy-start | bytes 786436

commit v2 on v1

v2 whole, which is shorter than its diff:
```python
import jax
import jax.numpy as jnp
from jax import lax
from jax.experimental import pallas as pl
from jax.experimental.pallas import tpu as pltpu
from jax.sharding import PartitionSpec as P

MESH = pl.DeviceIdType.MESH
CHUNKS = 8
BLOCK = 32
FAR_FIRST = (4, 3, 5, 2, 6, 1, 7)
NEAR_FIRST = (1, 7, 2, 6, 3, 5, 4)
F32 = jnp.float32
BF16 = jnp.bfloat16


def split(a):
    hi = a.astype(BF16)
    return hi, (a - hi.astype(F32)).astype(BF16)


def dot(a, b):
    return jnp.dot(a, b, preferred_element_type=F32)


def dot_rows(a, b):
    return lax.dot_general(a, b, (((1,), (1,)), ((), ())), preferred_element_type=F32)


def picked(tables, rows):
    n = rows.shape[1]
    high, low = rows // 128, rows % 128
    hot = (lax.broadcasted_iota(jnp.int32, (128, n), 0) == high).astype(BF16)
    mask = lax.broadcasted_iota(jnp.int32, (128, n), 0) == low
    out = []
    for table in tables:
        t = table.T
        first = t.astype(BF16)
        t = t - first.astype(F32)
        second = t.astype(BF16)
        third = (t - second.astype(F32)).astype(BF16)
        lines = (dot(first, hot) + dot(second, hot)) + dot(third, hot)
        out.append(jnp.sum(jnp.where(mask, lines, 0.0), axis=0, keepdims=True))
    return out


def exchange_kernel(
    op_hbm, ens_hbm, obs_ref, var_ref, rows_ref, fwd_all, ens_all, picks,
    op_v, ens_v, zsrc, zrecv, ysrc, yrecv,
    op_sem, ens_sem, own_sem,
    zs_sem, zr_sem, ys_sem, yr_sem, gs_sem, gr_sem,
    xs_sem, xr_sem, cs_sem, cr_sem,
    es_sem, er_sem, fs_sem, fr_sem,
):
    mem = lax.axis_index("mem")
    par = lax.axis_index("par")
    x, core = mem // 2, mem % 2
    y, z = par // 8, par % 8
    own = ens_hbm.shape[0]
    depth = op_hbm.shape[0] // CHUNKS
    twin = x * 2 + (1 - core)

    def at_z(d):
        return (mem, y * 8 + (z + d) % 8)

    def at_y(d):
        return (mem, ((y + d) % 8) * 8 + z)

    def mem_at(d):
        return ((x + d) % 4) * 2 + core

    def remote(src, dst, send, recv, device):
        copy = pltpu.make_async_remote_copy(
            src_ref=src, dst_ref=dst, send_sem=send, recv_sem=recv, device_id=device, device_id_type=MESH
        )
        copy.start()
        return copy

    barrier = pltpu.get_barrier_semaphore()
    friends = [at_z(d) for d in FAR_FIRST] + [at_y(d) for d in FAR_FIRST]
    friends += [(mem_at(d), par) for d in (2, 1, 3)] + [(twin, par)]
    for friend in friends:
        pl.semaphore_signal(barrier, inc=1, device_id=friend, device_id_type=MESH)

    ens_copy = pltpu.make_async_copy(ens_hbm, ens_v, ens_sem)
    ens_copy.start()
    op_copies = []
    for c in range(CHUNKS):
        lines = pl.ds(c * depth, depth)
        op_copies.append(pltpu.make_async_copy(op_hbm.at[lines], op_v.at[lines], op_sem.at[c]))
        op_copies[-1].start()

    own_rows = pl.ds(pl.multiple_of(mem * own, own), own)
    ens_copy.wait()
    own_copy = pltpu.make_async_copy(ens_v, ens_all.at[own_rows], own_sem)
    own_copy.start()

    total = jnp.zeros((own, op_hbm.shape[1]), F32)
    for c in range(CHUNKS):
        op_copies[c].wait()
        op_hi, op_lo = split(op_v[pl.ds(c * depth, depth), :])
        ens_hi, ens_lo = split(ens_v[:, pl.ds(c * depth, depth)])
        total += dot(ens_hi, op_hi) + dot(ens_lo, op_hi) + dot(ens_hi, op_lo)
    for q in range(8):
        zsrc[q] = total[(q // 4) * 16 : (q // 4) * 16 + 16, (q % 4) * 128 : (q % 4) * 128 + 128]

    pl.semaphore_wait(barrier, len(friends))

    z_out = {
        d: remote(zsrc.at[(z + d) % 8], zrecv.at[d], zs_sem.at[d], zr_sem.at[d], at_z(d)) for d in FAR_FIRST
    }
    ens_out = {
        d: remote(ens_hbm, ens_all.at[own_rows], es_sem.at[d], er_sem.at[d], (mem_at(d), par)) for d in (2, 1, 3)
    }
    twin_out = [remote(ens_hbm, ens_all.at[own_rows], fs_sem.at[0], fr_sem.at[0], (twin, par))]

    obs_rows, var_rows = picked((obs_ref[...], var_ref[...]), rows_ref[...])
    picks[...] = jnp.concatenate([obs_rows, var_rows] + [var_rows] * 6, axis=0)

    part = zsrc[z]
    for d in NEAR_FIRST:
        z_out[d].wait_recv()
        part += zrecv[d]
    ysrc[...] = part
    y_out = {d: remote(ysrc, yrecv.at[d], ys_sem.at[d], yr_sem.at[d], at_y(d)) for d in FAR_FIRST}
    for d in NEAR_FIRST:
        y_out[d].wait_recv()
        part += yrecv[d]
    fwd_all[mem, z] = part
    g_out = {
        d: remote(fwd_all.at[mem, z], fwd_all.at[mem, z], gs_sem.at[d], gr_sem.at[d], at_z(d)) for d in FAR_FIRST
    }

    x_out, c_out = {}, []

    def spread_piece(d):
        piece = fwd_all.at[mem, (z + 8 - d) % 8]
        for e in (2, 1, 3):
            x_out[e, d] = remote(piece, piece, xs_sem.at[e, d], xr_sem.at[e, d], (mem_at(e), par))
        c_out.append(remote(piece, piece, cs_sem.at[0, d], cr_sem.at[0, d], (twin, par)))

    def forward_ens(d):
        ens_out[d].wait_recv()
        lines = pl.ds(pl.multiple_of(((x + 4 - d) % 4) * 2 * own + core * own, own), own)
        twin_out.append(remote(ens_all.at[lines], ens_all.at[lines], fs_sem.at[d], fr_sem.at[d], (twin, par)))

    spread_piece(0)
    for d in NEAR_FIRST:
        g_out[d].wait_recv()
        spread_piece(d)
    forward_ens(1)
    forward_ens(3)
    for d in (0,) + NEAR_FIRST:
        for e in (1, 3, 2):
            x_out[e, d].wait_recv()
            piece = fwd_all.at[((x + 4 - e) % 4) * 2 + core, (z + 8 - d) % 8]
            c_out.append(remote(piece, piece, cs_sem.at[e, d], cr_sem.at[e, d], (twin, par)))
    forward_ens(2)
    for copy in c_out + twin_out:
        copy.wait()
    for group in (z_out, y_out, g_out, ens_out, x_out):
        for copy in group.values():
            copy.wait_send()
    own_copy.wait()


def exchange(operator, ensemble, obs, var, rows):
    own, params = ensemble.shape
    width = operator.shape[1]
    any_spec = pl.BlockSpec(memory_space=pl.ANY)
    vmem_spec = pl.BlockSpec(memory_space=pltpu.VMEM)
    dma = pltpu.SemaphoreType.DMA
    return pl.pallas_call(
        exchange_kernel,
        name="exchange",
        out_shape=(
            jax.ShapeDtypeStruct((8, 8, 16, 128), F32),
            jax.ShapeDtypeStruct((8 * own, params), F32),
            jax.ShapeDtypeStruct((8, width), F32),
        ),
        in_specs=[any_spec, any_spec, vmem_spec, vmem_spec, vmem_spec],
        out_specs=(vmem_spec, any_spec, vmem_spec),
        scratch_shapes=[
            pltpu.VMEM((params, width), F32),
            pltpu.VMEM((own, params), F32),
            pltpu.VMEM((8, 16, 128), F32),
            pltpu.VMEM((8, 16, 128), F32),
            pltpu.VMEM((16, 128), F32),
            pltpu.VMEM((8, 16, 128), F32),
            dma((CHUNKS,)), dma, dma,
            dma((8,)), dma((8,)), dma((8,)), dma((8,)), dma((8,)), dma((8,)),
            dma((4, 8)), dma((4, 8)), dma((4, 8)), dma((4, 8)),
            dma((4,)), dma((4,)), dma((4,)), dma((4,)),
        ],
        compiler_params=pltpu.CompilerParams(collective_id=0, has_side_effects=True),
    )(operator, ensemble, obs, var, rows)


def row_of(tile, i):
    return jnp.broadcast_to(tile[i:i+1, :], (8, 128))


def factor(m_ref, size, block):
    lanes = size // 128
    tiles = block // 8
    sub = lax.broadcasted_iota(jnp.int32, (8, 128), 0)
    lane = lax.broadcasted_iota(jnp.int32, (8, 128), 1)
    for k in range(size // block):
        base = k * block
        home, shift = base // 128, base % 128
        square = [m_ref[base + 8 * t: base + 8 * t + 8, home * 128: home * 128 + 128] for t in range(tiles)]
        panel = []
        for t in range(tiles):
            line = []
            for l in range(lanes):
                v = m_ref[base + 8 * t: base + 8 * t + 8, l * 128: l * 128 + 128]
                if l == home:
                    inside = (lane >= shift) & (lane < shift + block)
                    v = jnp.where(inside, (lane - shift == sub + 8 * t).astype(F32), v)
                line.append(v)
            panel.append(line)
        done = [[None] * lanes for _ in range(tiles)]
        cols = []
        for j in range(block):
            first = j // 8
            col = [jnp.broadcast_to(square[t][:, shift + j: shift + j + 1], (8, 128)) for t in range(first, tiles)]
            for p in range(j):
                scale = row_of(cols[p][first - p // 8], j % 8)
                for t in range(first, tiles):
                    col[t - first] = col[t - first] - cols[p][t - p // 8] * scale
            inv = lax.rsqrt(row_of(col[0], j % 8))
            col = [c * inv for c in col]
            cols.append(col)
            below = jnp.where(sub > j % 8, col[0], 0.0)
            for l in range(lanes):
                line = row_of(panel[first][l], j % 8) * inv
                old = done[first][l]
                done[first][l] = line if old is None else jnp.where(sub >= j % 8, line, old)
                for t in range(first, tiles):
                    panel[t][l] = panel[t][l] - (below if t == first else col[t - first]) * line
        z = jnp.concatenate([jnp.concatenate(done[t], axis=1) for t in range(tiles)], axis=0)
        m_ref[base: base + block, :] = z
        after = base + block
        if after < size:
            hi, lo = split(z)
            left = jnp.concatenate([hi, hi, lo], axis=0).T
            right = jnp.concatenate([hi, lo, hi], axis=0)
            update = jnp.dot(left[after:], right, preferred_element_type=F32)
            rest = m_ref[after:, :]
            col_id = lax.broadcasted_iota(jnp.int32, rest.shape, 1)
            rest = jnp.where((col_id >= base) & (col_id < after), 0.0, rest)
            m_ref[after:, :] = rest - update


def dot3(a, b, product=dot):
    a_hi, a_lo = split(a)
    b_hi, b_lo = split(b)
    return product(a_hi, b_hi) + product(a_lo, b_hi) + product(a_hi, b_lo)


def update_kernel(fwd_ref, ens_all, ens_ref, noise_ref, picks_ref, out_ref, ens_v, m_ref, ens_sem):
    mem = lax.axis_index("mem")
    ens_copy = pltpu.make_async_copy(ens_all, ens_v, ens_sem)
    ens_copy.start()

    def rows_of(m):
        halves = [jnp.concatenate([fwd_ref[m, h * 4 + l] for l in range(4)], axis=1) for h in range(2)]
        return jnp.concatenate(halves, axis=0)

    forward = jnp.concatenate([rows_of(m) for m in range(8)], axis=0)
    members = forward.shape[0]
    obs_rows, var_rows = picks_ref[0:1, :], picks_ref[1:2, :]
    scale = lax.rsqrt(var_rows)
    spread = (forward - jnp.mean(forward, axis=0, keepdims=True)) * scale
    residual = (obs_rows + jnp.sqrt(var_rows) * noise_ref[...] - rows_of(mem)) * scale
    both = (members, members)
    eye = (lax.broadcasted_iota(jnp.int32, both, 0) == lax.broadcasted_iota(jnp.int32, both, 1)).astype(F32)
    m_ref[...] = dot3(spread, spread, dot_rows) + (members - 1) * eye
    factor(m_ref, members, BLOCK)
    cross = dot3(residual, spread, dot_rows)
    lower = lax.broadcasted_iota(jnp.int32, both, 0) >= lax.broadcasted_iota(jnp.int32, both, 1)
    inverse = jnp.where(lower, m_ref[...], 0.0)
    weights = dot3(dot3(cross, inverse, dot_rows), inverse)
    weights = weights - jnp.mean(weights, axis=1, keepdims=True)
    ens_copy.wait()
    step = 512
    for c in range(out_ref.shape[1] // step):
        part = pl.ds(c * step, step)
        out_ref[:, part] = ens_ref[:, part] + dot3(weights, ens_v[:, part])


def update(pieces, gathered, ensemble, noise, picks):
    vmem_spec = pl.BlockSpec(memory_space=pltpu.VMEM)
    return pl.pallas_call(
        update_kernel,
        name="update",
        out_shape=jax.ShapeDtypeStruct(ensemble.shape, F32),
        in_specs=[vmem_spec, pl.BlockSpec(memory_space=pl.ANY), vmem_spec, vmem_spec, vmem_spec],
        out_specs=vmem_spec,
        scratch_shapes=[
            pltpu.VMEM(gathered.shape, F32),
            pltpu.VMEM((gathered.shape[0],) * 2, F32),
            pltpu.SemaphoreType.DMA,
        ],
    )(pieces, gathered, ensemble, noise, picks)


def per_device(operator, ensemble, noise, observations, variances, rows):
    obs, var = observations.reshape(128, 128), variances.reshape(128, 128)
    pieces, gathered, picks = exchange(operator, ensemble, obs, var, rows.reshape(1, -1))
    return update(pieces, gathered, ensemble, noise, picks)


def solution(mesh):
    return jax.shard_map(
        per_device,
        mesh=mesh,
        in_specs=(P("par", None), P("mem", "par"), P("mem", None), P(), P(), P()),
        out_specs=P("mem", "par"),
        check_vma=False,
    )
```

time: 115 us -> 48.3 us (0.42)
  other arithmetic: 58 us -> 0 us
  local copies, waits for them, and re-layouts: 10.7 us -> 0 us
  Pallas kernels: 39.2 us -> 48.1 us
  matrix products: 4.99 us -> 0 us
  between operations: 1.54 us -> 0.01 us
    another operation x9 -> x0, other arithmetic: 53.8 us -> none  [the longest x6 34.1 us: cholesky_solve(): factor = jnp.linalg.cholesky(matrix)]
    pallas_call x0 -> x1, Pallas kernels: none -> 9.4 us  [update(): pl.pallas_call(update_kernel, name='update', out_shape=jax.ShapeDtypeStru...]
    gather x2 -> x0, local copies, waits for them, and re-layouts: 6.28 us -> none  [the longest x1 3.14 us: per_device(): var_rows = jnp.take(variances, rows)]
    another operation x9 -> x0, local copies, waits for them, and re-layouts: 3.92 us -> none
    dot_general x3 -> x0, matrix products: 3.25 us -> none  [the longest x1 2.06 us: per_device(): jnp.dot(weights.T, deviation, precision=highest, preferred_element_type=j...]
    reduce_sum x2 -> x0, other arithmetic: 3.13 us -> none  [the longest x1 1.74 us: per_device(): deviation = gathered - jnp.mean(gathered, axis=0, keepdims=True)]
    another operation x8 -> x0, matrix products: 1.74 us -> none  [the longest x3 0.65 us: cholesky_solve(): lax.linalg.triangular_solve(factor, right, left_side=True, lower=True)]
where the time goes in v2:
time: 48.3 us; the launch traced here: 48.1 us
  Pallas kernels  48.1 us (100%)
    pallas_call x1, Pallas kernels, exchange(): pl.pallas_call(exchange_kernel, name='exchange', out_shape=(jax.ShapeDtyp...  38.7 us
    pallas_call x1, Pallas kernels, update(): pl.pallas_call(update_kernel, name='update', out_shape=jax.ShapeDtypeStru...  9.4 us

profile of v2, /device:TPU:1, one launch (start us, length us, event | category | flops | bytes accessed | tf_op | source)
XLA Modules:
  0.0 48.1 jit_solution(18165911402617285747)
XLA Ops:
  0.0 38.7 %exchange.1 = (f32[8,8,16,128]{3,2,1,0:T(8,128)}, f32[256,2048]{1,0:T(8,128)}, f32[8,512]{1,0:T(8,128)}) custom-call(f32[2048,512]{1,0:T(8,128)} %op_hbm.1, f32[32,2048]{1,0:T(8,128)} %ens_ref.1, f32[128,128]{1,0:T(8,128)} %bitcast.3, f32[128,128]{1,0:T(8,128)} %bitcast.4, s32[1,512]{1,0:T(1,128)} %bitcast.5), custom_call_target="tpu_custom_call" | custom-call | tf_op jit(solution)/shard_map/exchange/pallas_call | solution.py:173
  38.7 9.4 %update.1 = f32[32,2048]{1,0:T(8,128)} custom-call(f32[8,8,16,128]{3,2,1,0:T(8,128)} %get-tuple-element.8.fwd_ref, f32[256,2048]{1,0:T(8,128)} %get-tuple-element.9.ens_all, f32[32,2048]{1,0:T(8,128)} %ens_ref.1, f32[32,512]{1,0:T(8,128)} %noise_ref.1, f32[8,512]{1,0:T(8,128)} %get-tuple-element.10.picks_ref), custom_call_target="tpu_custom_call" | custom-call | tf_op jit(solution)/shard_map/update/pallas_call | solution.py:294

commit v3 on v2

--- a/solution.py
+++ b/solution.py
@@ -6,10 +6,12 @@
 from jax.sharding import PartitionSpec as P
 
 MESH = pl.DeviceIdType.MESH
-CHUNKS = 8
+CHUNKS = 4
 BLOCK = 32
+FRONTS = {0: (0, 16), 12: (16, 32)}
 FAR_FIRST = (4, 3, 5, 2, 6, 1, 7)
-NEAR_FIRST = (1, 7, 2, 6, 3, 5, 4)
+NEAR = (1, 7, 2, 6)
+FAR = (4, 3, 5)
 F32 = jnp.float32
 BF16 = jnp.bfloat16
 
@@ -45,12 +47,9 @@
 
 
 def exchange_kernel(
-    op_hbm, ens_hbm, obs_ref, var_ref, rows_ref, fwd_all, ens_all, picks,
-    op_v, ens_v, zsrc, zrecv, ysrc, yrecv,
-    op_sem, ens_sem, own_sem,
-    zs_sem, zr_sem, ys_sem, yr_sem, gs_sem, gr_sem,
-    xs_sem, xr_sem, cs_sem, cr_sem,
-    es_sem, er_sem, fs_sem, fr_sem,
+    op_hbm, ens_hbm, obs_hbm, var_hbm, rows_hbm, fwd_all, ens_all, picks,
+    op_v, ens_v, obs_v, var_v, rows_v, source, came_one, middle, came_two,
+    op_sem, load_sem, own_sem, send_sem, one_r, two_r, three_r, x_r, twin_r, ens_r, ens_twin_r,
 ):
     mem = lax.axis_index("mem")
     par = lax.axis_index("par")
@@ -69,26 +68,38 @@
     def mem_at(d):
         return ((x + d) % 4) * 2 + core
 
-    def remote(src, dst, send, recv, device):
-        copy = pltpu.make_async_remote_copy(
+    across, along, place = (at_z, at_y), (at_y, at_z), (z, y)
+
+    def copy_to(src, dst, send, recv, device):
+        return pltpu.make_async_remote_copy(
             src_ref=src, dst_ref=dst, send_sem=send, recv_sem=recv, device_id=device, device_id_type=MESH
         )
-        copy.start()
-        return copy
+
+    def arrived(ref, recv):
+        copy_to(ref, ref, send_sem.at[0], recv, (twin, par)).wait_recv()
+
+    def sent(ref, send):
+        copy_to(ref, ref, send, one_r.at[0], (twin, par)).wait_send()
 
     barrier = pltpu.get_barrier_semaphore()
-    friends = [at_z(d) for d in FAR_FIRST] + [at_y(d) for d in FAR_FIRST]
+    friends = [at(d) for d in FAR_FIRST for at in across]
     friends += [(mem_at(d), par) for d in (2, 1, 3)] + [(twin, par)]
     for friend in friends:
         pl.semaphore_signal(barrier, inc=1, device_id=friend, device_id_type=MESH)
 
-    ens_copy = pltpu.make_async_copy(ens_hbm, ens_v, ens_sem)
+    ens_copy = pltpu.make_async_copy(ens_hbm, ens_v, load_sem.at[0])
     ens_copy.start()
     op_copies = []
     for c in range(CHUNKS):
         lines = pl.ds(c * depth, depth)
         op_copies.append(pltpu.make_async_copy(op_hbm.at[lines], op_v.at[lines], op_sem.at[c]))
         op_copies[-1].start()
+    small = [
+        pltpu.make_async_copy(src, dst, load_sem.at[i])
+        for i, src, dst in ((1, obs_hbm, obs_v), (2, var_hbm, var_v), (3, rows_hbm, rows_v))
+    ]
+    for copy in small:
+        copy.start()
 
     own_rows = pl.ds(pl.multiple_of(mem * own, own), own)
     ens_copy.wait()
@@ -101,66 +112,90 @@
         op_hi, op_lo = split(op_v[pl.ds(c * depth, depth), :])
         ens_hi, ens_lo = split(ens_v[:, pl.ds(c * depth, depth)])
         total += dot(ens_hi, op_hi) + dot(ens_lo, op_hi) + dot(ens_hi, op_lo)
-    for q in range(8):
-        zsrc[q] = total[(q // 4) * 16 : (q // 4) * 16 + 16, (q % 4) * 128 : (q % 4) * 128 + 128]
+    for h in range(2):
+        for q in range(8):
+            top, left = (q // 2) * 8, h * 256 + (q % 2) * 128
+            source[h, q] = total[top : top + 8, left : left + 128]
 
     pl.semaphore_wait(barrier, len(friends))
 
-    z_out = {
-        d: remote(zsrc.at[(z + d) % 8], zrecv.at[d], zs_sem.at[d], zr_sem.at[d], at_z(d)) for d in FAR_FIRST
-    }
-    ens_out = {
-        d: remote(ens_hbm, ens_all.at[own_rows], es_sem.at[d], er_sem.at[d], (mem_at(d), par)) for d in (2, 1, 3)
-    }
-    twin_out = [remote(ens_hbm, ens_all.at[own_rows], fs_sem.at[0], fr_sem.at[0], (twin, par))]
-
-    obs_rows, var_rows = picked((obs_ref[...], var_ref[...]), rows_ref[...])
+    for d in FAR_FIRST:
+        for h in range(2):
+            piece = source.at[h, (place[h] + d) % 8]
+            copy_to(piece, came_one.at[h, d], send_sem.at[0], one_r.at[h], across[h](d)).start()
+    for d in (1, 3):
+        copy_to(ens_hbm, ens_all.at[own_rows], send_sem.at[3], ens_r.at[d], (mem_at(d), par)).start()
+    copy_to(ens_hbm, ens_all.at[own_rows], send_sem.at[4], ens_twin_r, (twin, par)).start()
+
+    for copy in small:
+        copy.wait()
+    obs_rows, var_rows = picked((obs_v[...], var_v[...]), rows_v[...])
     picks[...] = jnp.concatenate([obs_rows, var_rows] + [var_rows] * 6, axis=0)
 
-    part = zsrc[z]
-    for d in NEAR_FIRST:
-        z_out[d].wait_recv()
-        part += zrecv[d]
-    ysrc[...] = part
-    y_out = {d: remote(ysrc, yrecv.at[d], ys_sem.at[d], yr_sem.at[d], at_y(d)) for d in FAR_FIRST}
-    for d in NEAR_FIRST:
-        y_out[d].wait_recv()
-        part += yrecv[d]
-    fwd_all[mem, z] = part
-    g_out = {
-        d: remote(fwd_all.at[mem, z], fwd_all.at[mem, z], gs_sem.at[d], gr_sem.at[d], at_z(d)) for d in FAR_FIRST
-    }
-
-    x_out, c_out = {}, []
-
-    def spread_piece(d):
-        piece = fwd_all.at[mem, (z + 8 - d) % 8]
+    others = pl.ds(1, 7)
+    part = [None, None]
+    for h in range(2):
+        arrived(came_one.at[h, others], one_r.at[h])
+        part[h] = source[h, place[h]]
+        for d in range(1, 8):
+            part[h] += came_one[h, d]
+        middle[h] = part[h]
+        for d in FAR_FIRST:
+            copy_to(middle.at[h], came_two.at[h, d], send_sem.at[1], two_r.at[h], along[h](d)).start()
+    for h in range(2):
+        arrived(came_two.at[h, others], two_r.at[h])
+        for d in range(1, 8):
+            part[h] += came_two[h, d]
+        fwd_all[mem, h, place[h]] = part[h]
+        piece = fwd_all.at[mem, h, place[h]]
+        for d in FAR_FIRST:
+            copy_to(piece, piece, send_sem.at[2], three_r.at[int(d in FAR), h], across[h](d)).start()
+
+    def spread_piece(h, d):
+        piece = fwd_all.at[mem, h, (place[h] + 8 - d) % 8]
         for e in (2, 1, 3):
-            x_out[e, d] = remote(piece, piece, xs_sem.at[e, d], xr_sem.at[e, d], (mem_at(e), par))
-        c_out.append(remote(piece, piece, cs_sem.at[0, d], cr_sem.at[0, d], (twin, par)))
-
-    def forward_ens(d):
-        ens_out[d].wait_recv()
-        lines = pl.ds(pl.multiple_of(((x + 4 - d) % 4) * 2 * own + core * own, own), own)
-        twin_out.append(remote(ens_all.at[lines], ens_all.at[lines], fs_sem.at[d], fr_sem.at[d], (twin, par)))
-
-    spread_piece(0)
-    for d in NEAR_FIRST:
-        g_out[d].wait_recv()
-        spread_piece(d)
-    forward_ens(1)
-    forward_ens(3)
-    for d in (0,) + NEAR_FIRST:
-        for e in (1, 3, 2):
-            x_out[e, d].wait_recv()
-            piece = fwd_all.at[((x + 4 - e) % 4) * 2 + core, (z + 8 - d) % 8]
-            c_out.append(remote(piece, piece, cs_sem.at[e, d], cr_sem.at[e, d], (twin, par)))
-    forward_ens(2)
-    for copy in c_out + twin_out:
-        copy.wait()
-    for group in (z_out, y_out, g_out, ens_out, x_out):
-        for copy in group.values():
-            copy.wait_send()
+            copy_to(piece, piece, send_sem.at[5], x_r.at[int(d in FAR)], (mem_at(e), par)).start()
+        copy_to(piece, piece, send_sem.at[6], twin_r, (twin, par)).start()
+
+    def ens_rows(d, first, count):
+        return pl.ds(pl.multiple_of(((x + 4 - d) % 4) * 2 * own + core * own + first, count), count)
+
+    def ens_to_twin(lines):
+        copy_to(ens_all.at[lines], ens_all.at[lines], send_sem.at[4], ens_twin_r, (twin, par)).start()
+
+    half = own // 2
+    for h in range(2):
+        spread_piece(h, 0)
+    for i, d in ((0, 1), (1, 3)):
+        arrived(ens_all.at[ens_rows(d, 0, own)], ens_r.at[d])
+        lines = ens_rows(d, i * half, half)
+        copy_to(ens_all.at[lines], ens_all.at[lines], send_sem.at[3], ens_r.at[2 * i], (mem_at(d), par)).start()
+        ens_to_twin(ens_rows(d, 0, own))
+    for far, group in enumerate((NEAR, FAR)):
+        for h in range(2):
+            arrived(fwd_all.at[mem, h, pl.ds(0, len(group))], three_r.at[far, h])
+            for d in group:
+                spread_piece(h, d)
+    for i in range(2):
+        lines = ens_rows(2, i * half, half)
+        arrived(ens_all.at[lines], ens_r.at[2 * i])
+        ens_to_twin(lines)
+    for far, group in enumerate(((0,) + NEAR, FAR)):
+        arrived(fwd_all.at[pl.ds(0, 3), :, pl.ds(0, len(group))], x_r.at[far])
+        for d in group:
+            for h in range(2):
+                for e in (1, 3, 2):
+                    piece = fwd_all.at[((x + 4 - e) % 4) * 2 + core, h, (place[h] + 8 - d) % 8]
+                    copy_to(piece, piece, send_sem.at[6], twin_r, (twin, par)).start()
+    arrived(fwd_all.at[pl.ds(0, 4)], twin_r)
+    arrived(ens_all.at[pl.ds(0, 4 * own)], ens_twin_r)
+    for i in range(2):
+        sent(came_one.at[:, others], send_sem.at[i])
+    sent(came_one.at[:, others], send_sem.at[2])
+    sent(ens_all.at[pl.ds(0, 3 * own)], send_sem.at[3])
+    sent(ens_all.at[pl.ds(0, 4 * own)], send_sem.at[4])
+    sent(fwd_all.at[pl.ds(0, 3)], send_sem.at[5])
+    sent(fwd_all.at[pl.ds(0, 4)], send_sem.at[6])
     own_copy.wait()
 
 
@@ -174,23 +209,24 @@
         exchange_kernel,
         name="exchange",
         out_shape=(
-            jax.ShapeDtypeStruct((8, 8, 16, 128), F32),
+            jax.ShapeDtypeStruct((8, 2, 8, 8, 128), F32),
             jax.ShapeDtypeStruct((8 * own, params), F32),
             jax.ShapeDtypeStruct((8, width), F32),
         ),
-        in_specs=[any_spec, any_spec, vmem_spec, vmem_spec, vmem_spec],
+        in_specs=[any_spec] * 5,
         out_specs=(vmem_spec, any_spec, vmem_spec),
         scratch_shapes=[
             pltpu.VMEM((params, width), F32),
             pltpu.VMEM((own, params), F32),
-            pltpu.VMEM((8, 16, 128), F32),
-            pltpu.VMEM((8, 16, 128), F32),
-            pltpu.VMEM((16, 128), F32),
-            pltpu.VMEM((8, 16, 128), F32),
-            dma((CHUNKS,)), dma, dma,
-            dma((8,)), dma((8,)), dma((8,)), dma((8,)), dma((8,)), dma((8,)),
-            dma((4, 8)), dma((4, 8)), dma((4, 8)), dma((4, 8)),
-            dma((4,)), dma((4,)), dma((4,)), dma((4,)),
+            pltpu.VMEM(obs.shape, F32),
+            pltpu.VMEM(var.shape, F32),
+            pltpu.VMEM(rows.shape, rows.dtype),
+            pltpu.VMEM((2, 8, 8, 128), F32),
+            pltpu.VMEM((2, 8, 8, 128), F32),
+            pltpu.VMEM((2, 8, 128), F32),
+            pltpu.VMEM((2, 8, 8, 128), F32),
+            dma((CHUNKS,)), dma((4,)), dma, dma((7,)),
+            dma((2,)), dma((2,)), dma((2, 2)), dma((2,)), dma, dma((4,)), dma,
         ],
         compiler_params=pltpu.CompilerParams(collective_id=0, has_side_effects=True),
     )(operator, ensemble, obs, var, rows)
@@ -208,34 +244,44 @@
     for k in range(size // block):
         base = k * block
         home, shift = base // 128, base % 128
-        square = [m_ref[base + 8 * t: base + 8 * t + 8, home * 128: home * 128 + 128] for t in range(tiles)]
         panel = []
         for t in range(tiles):
-            line = []
-            for l in range(lanes):
-                v = m_ref[base + 8 * t: base + 8 * t + 8, l * 128: l * 128 + 128]
-                if l == home:
-                    inside = (lane >= shift) & (lane < shift + block)
-                    v = jnp.where(inside, (lane - shift == sub + 8 * t).astype(F32), v)
-                line.append(v)
+            line = [m_ref[base + 8 * t: base + 8 * t + 8, l * 128: l * 128 + 128] for l in range(lanes)]
+            line.append(line[home])
+            inside = (lane >= shift) & (lane < shift + block)
+            line[home] = jnp.where(inside, (lane - shift == sub + 8 * t).astype(F32), line[home])
             panel.append(line)
         done = [[None] * lanes for _ in range(tiles)]
-        cols = []
+        cols, raw, invs, fronts, seen = [], [], [], {}, {}
         for j in range(block):
+            if j in FRONTS:
+                lo_c, hi_c = FRONTS[j]
+                for c in range(lo_c, hi_c):
+                    fronts[c] = [jnp.broadcast_to(panel[t][lanes][:, shift + c: shift + c + 1], (8, 128)) for t in range(c // 8, tiles)]
+                    seen[c] = j
             first = j // 8
-            col = [jnp.broadcast_to(square[t][:, shift + j: shift + j + 1], (8, 128)) for t in range(first, tiles)]
-            for p in range(j):
-                scale = row_of(cols[p][first - p // 8], j % 8)
-                for t in range(first, tiles):
-                    col[t - first] = col[t - first] - cols[p][t - p // 8] * scale
-            inv = lax.rsqrt(row_of(col[0], j % 8))
+            col = fronts[j]
+            for p in range(seen[j], j):
+                if p == j - 1:
+                    scale = row_of(raw[p][first - p // 8], j % 8)
+                    for t in range(first, tiles):
+                        col[t - first] = col[t - first] - raw[p][t - p // 8] * scale * invs[p]
+                else:
+                    scale = row_of(cols[p][first - p // 8], j % 8)
+                    for t in range(first, tiles):
+                        col[t - first] = col[t - first] - cols[p][t - p // 8] * scale
+            raw.append(col)
+            pivot = row_of(col[0], j % 8)
+            invs.append(1.0 / pivot)
+            inv = lax.rsqrt(pivot)
             col = [c * inv for c in col]
             cols.append(col)
             below = jnp.where(sub > j % 8, col[0], 0.0)
-            for l in range(lanes):
+            for l in range(lanes + 1 if j < max(FRONTS) else lanes):
                 line = row_of(panel[first][l], j % 8) * inv
-                old = done[first][l]
-                done[first][l] = line if old is None else jnp.where(sub >= j % 8, line, old)
+                if l < lanes:
+                    old = done[first][l]
+                    done[first][l] = line if old is None else jnp.where(sub >= j % 8, line, old)
                 for t in range(first, tiles):
                     panel[t][l] = panel[t][l] - (below if t == first else col[t - first]) * line
         z = jnp.concatenate([jnp.concatenate(done[t], axis=1) for t in range(tiles)], axis=0)
@@ -264,8 +310,8 @@
     ens_copy.start()
 
     def rows_of(m):
-        halves = [jnp.concatenate([fwd_ref[m, h * 4 + l] for l in range(4)], axis=1) for h in range(2)]
-        return jnp.concatenate(halves, axis=0)
+        lines = [[fwd_ref[m, h, r * 2 + l] for h in range(2) for l in range(2)] for r in range(4)]
+        return jnp.concatenate([jnp.concatenate(line, axis=1) for line in lines], axis=0)
 
     forward = jnp.concatenate([rows_of(m) for m in range(8)], axis=0)
     members = forward.shape[0]

time: 48.3 us -> 44.5 us (0.921)
  Pallas kernels: 48.1 us -> 44.4 us
    pallas_call x1, Pallas kernels: 38.7 us -> 35.7 us  [exchange(): pl.pallas_call(exchange_kernel, name='exchange', out_shape=(jax.ShapeDtyp...]
    pallas_call x1, Pallas kernels: 9.4 us -> 8.67 us  [update(): pl.pallas_call(update_kernel, name='update', out_shape=jax.ShapeDtypeStru...]
where the time goes in v3:
time: 44.5 us; the launch traced here: 44.4 us
  Pallas kernels  44.4 us (100%)
    pallas_call x1, Pallas kernels, exchange(): pl.pallas_call(exchange_kernel, name='exchange', out_shape=(jax.ShapeDtyp...  35.7 us
    pallas_call x1, Pallas kernels, update(): pl.pallas_call(update_kernel, name='update', out_shape=jax.ShapeDtypeStru...  8.67 us

profile of v3, /device:TPU:1, one launch (start us, length us, event | category | flops | bytes accessed | tf_op | source)
XLA Modules:
  0.0 44.4 jit_solution(13023257756129577632)
XLA Ops:
  0.0 35.7 %exchange.1 = (f32[8,2,8,8,128]{4,3,2,1,0:T(8,128)}, f32[256,2048]{1,0:T(8,128)}, f32[8,512]{1,0:T(8,128)}) custom-call(f32[2048,512]{1,0:T(8,128)} %op_hbm.1, f32[32,2048]{1,0:T(8,128)} %ens_ref.1, f32[128,128]{1,0:T(8,128)} %bitcast.3, f32[128,128]{1,0:T(8,128)} %bitcast.4, s32[1,512]{1,0:T(1,128)} %bitcast.5), custom_call_target="tpu_custom_call" | custom-call | tf_op jit(solution)/shard_map/exchange/pallas_call | solution.py:208
  35.7 8.7 %update.1 = f32[32,2048]{1,0:T(8,128)} custom-call(f32[8,2,8,8,128]{4,3,2,1,0:T(8,128)} %get-tuple-element.8.fwd_ref, f32[256,2048]{1,0:T(8,128)} %get-tuple-element.9.ens_all, f32[32,2048]{1,0:T(8,128)} %ens_ref.1, f32[32,512]{1,0:T(8,128)} %noise_ref.1, f32[8,512]{1,0:T(8,128)} %get-tuple-element.10.picks_ref), custom_call_target="tpu_custom_call" | custom-call | tf_op jit(solution)/shard_map/update/pallas_call | solution.py:340

commit v4 on v3

--- a/solution.py
+++ b/solution.py
@@ -48,8 +48,8 @@
 
 def exchange_kernel(
     op_hbm, ens_hbm, obs_hbm, var_hbm, rows_hbm, fwd_all, ens_all, picks,
-    op_v, ens_v, obs_v, var_v, rows_v, source, came_one, middle, came_two,
-    op_sem, load_sem, own_sem, send_sem, one_r, two_r, three_r, x_r, twin_r, ens_r, ens_twin_r,
+    op_v, obs_v, var_v, rows_v, source, came_one, middle, came_two,
+    op_sem, load_sem, send_sem, one_r, two_r, three_r, x_r, twin_r, ens_r, ens_twin_r,
 ):
     mem = lax.axis_index("mem")
     par = lax.axis_index("par")
@@ -87,7 +87,9 @@
     for friend in friends:
         pl.semaphore_signal(barrier, inc=1, device_id=friend, device_id_type=MESH)
 
-    ens_copy = pltpu.make_async_copy(ens_hbm, ens_v, load_sem.at[0])
+    own_rows = pl.ds(pl.multiple_of(mem * own, own), own)
+    own_ens = ens_all.at[own_rows]
+    ens_copy = pltpu.make_async_copy(ens_hbm, own_ens, load_sem.at[0])
     ens_copy.start()
     op_copies = []
     for c in range(CHUNKS):
@@ -101,16 +103,13 @@
     for copy in small:
         copy.start()
 
-    own_rows = pl.ds(pl.multiple_of(mem * own, own), own)
     ens_copy.wait()
-    own_copy = pltpu.make_async_copy(ens_v, ens_all.at[own_rows], own_sem)
-    own_copy.start()
 
     total = jnp.zeros((own, op_hbm.shape[1]), F32)
     for c in range(CHUNKS):
         op_copies[c].wait()
         op_hi, op_lo = split(op_v[pl.ds(c * depth, depth), :])
-        ens_hi, ens_lo = split(ens_v[:, pl.ds(c * depth, depth)])
+        ens_hi, ens_lo = split(ens_all[own_rows, pl.ds(c * depth, depth)])
         total += dot(ens_hi, op_hi) + dot(ens_lo, op_hi) + dot(ens_hi, op_lo)
     for h in range(2):
         for q in range(8):
@@ -124,8 +123,8 @@
             piece = source.at[h, (place[h] + d) % 8]
             copy_to(piece, came_one.at[h, d], send_sem.at[0], one_r.at[h], across[h](d)).start()
     for d in (1, 3):
-        copy_to(ens_hbm, ens_all.at[own_rows], send_sem.at[3], ens_r.at[d], (mem_at(d), par)).start()
-    copy_to(ens_hbm, ens_all.at[own_rows], send_sem.at[4], ens_twin_r, (twin, par)).start()
+        copy_to(own_ens, own_ens, send_sem.at[3], ens_r.at[d], (mem_at(d), par)).start()
+    copy_to(own_ens, own_ens, send_sem.at[4], ens_twin_r, (twin, par)).start()
 
     for copy in small:
         copy.wait()
@@ -196,7 +195,6 @@
     sent(ens_all.at[pl.ds(0, 4 * own)], send_sem.at[4])
     sent(fwd_all.at[pl.ds(0, 3)], send_sem.at[5])
     sent(fwd_all.at[pl.ds(0, 4)], send_sem.at[6])
-    own_copy.wait()
 
 
 def exchange(operator, ensemble, obs, var, rows):
@@ -209,15 +207,14 @@
         exchange_kernel,
         name="exchange",
         out_shape=(
-            jax.ShapeDtypeStruct((8, 2, 8, 8, 128), F32),
-            jax.ShapeDtypeStruct((8 * own, params), F32),
-            jax.ShapeDtypeStruct((8, width), F32),
+            pltpu.VMEM((8, 2, 8, 8, 128), F32),
+            pltpu.VMEM((8 * own, params), F32),
+            pltpu.VMEM((8, width), F32),
         ),
         in_specs=[any_spec] * 5,
-        out_specs=(vmem_spec, any_spec, vmem_spec),
+        out_specs=(vmem_spec,) * 3,
         scratch_shapes=[
             pltpu.VMEM((params, width), F32),
-            pltpu.VMEM((own, params), F32),
             pltpu.VMEM(obs.shape, F32),
             pltpu.VMEM(var.shape, F32),
             pltpu.VMEM(rows.shape, rows.dtype),
@@ -225,7 +222,7 @@
             pltpu.VMEM((2, 8, 8, 128), F32),
             pltpu.VMEM((2, 8, 128), F32),
             pltpu.VMEM((2, 8, 8, 128), F32),
-            dma((CHUNKS,)), dma((4,)), dma, dma((7,)),
+            dma((CHUNKS,)), dma((4,)), dma((7,)),
             dma((2,)), dma((2,)), dma((2, 2)), dma((2,)), dma, dma((4,)), dma,
         ],
         compiler_params=pltpu.CompilerParams(collective_id=0, has_side_effects=True),
@@ -304,10 +301,11 @@
     return product(a_hi, b_hi) + product(a_lo, b_hi) + product(a_hi, b_lo)
 
 
-def update_kernel(fwd_ref, ens_all, ens_ref, noise_ref, picks_ref, out_ref, ens_v, m_ref, ens_sem):
+def update_kernel(fwd_ref, ens_ref, noise_hbm, picks_ref, out_ref, noise_v, m_ref, noise_sem):
     mem = lax.axis_index("mem")
-    ens_copy = pltpu.make_async_copy(ens_all, ens_v, ens_sem)
-    ens_copy.start()
+    own = out_ref.shape[0]
+    noise_copy = pltpu.make_async_copy(noise_hbm, noise_v, noise_sem)
+    noise_copy.start()
 
     def rows_of(m):
         lines = [[fwd_ref[m, h, r * 2 + l] for h in range(2) for l in range(2)] for r in range(4)]
@@ -318,43 +316,49 @@
     obs_rows, var_rows = picks_ref[0:1, :], picks_ref[1:2, :]
     scale = lax.rsqrt(var_rows)
     spread = (forward - jnp.mean(forward, axis=0, keepdims=True)) * scale
-    residual = (obs_rows + jnp.sqrt(var_rows) * noise_ref[...] - rows_of(mem)) * scale
     both = (members, members)
     eye = (lax.broadcasted_iota(jnp.int32, both, 0) == lax.broadcasted_iota(jnp.int32, both, 1)).astype(F32)
     m_ref[...] = dot3(spread, spread, dot_rows) + (members - 1) * eye
     factor(m_ref, members, BLOCK)
+    noise_copy.wait()
+    residual = (obs_rows + jnp.sqrt(var_rows) * noise_v[...] - rows_of(mem)) * scale
     cross = dot3(residual, spread, dot_rows)
     lower = lax.broadcasted_iota(jnp.int32, both, 0) >= lax.broadcasted_iota(jnp.int32, both, 1)
     inverse = jnp.where(lower, m_ref[...], 0.0)
     weights = dot3(dot3(cross, inverse, dot_rows), inverse)
     weights = weights - jnp.mean(weights, axis=1, keepdims=True)
-    ens_copy.wait()
+    own_rows = pl.ds(pl.multiple_of(mem * own, own), own)
     step = 512
     for c in range(out_ref.shape[1] // step):
         part = pl.ds(c * step, step)
-        out_ref[:, part] = ens_ref[:, part] + dot3(weights, ens_v[:, part])
-
-
-def update(pieces, gathered, ensemble, noise, picks):
+        out_ref[:, part] = ens_ref[own_rows, part] + dot3(weights, ens_ref[:, part])
+
+
+def update(pieces, gathered, noise, picks):
+    pieces, gathered, picks = (
+        pltpu.with_memory_space_constraint(a, pltpu.VMEM) for a in (pieces, gathered, picks)
+    )
+    members, params = gathered.shape
+    own = noise.shape[0]
     vmem_spec = pl.BlockSpec(memory_space=pltpu.VMEM)
     return pl.pallas_call(
         update_kernel,
         name="update",
-        out_shape=jax.ShapeDtypeStruct(ensemble.shape, F32),
-        in_specs=[vmem_spec, pl.BlockSpec(memory_space=pl.ANY), vmem_spec, vmem_spec, vmem_spec],
+        out_shape=jax.ShapeDtypeStruct((own, params), F32),
+        in_specs=[vmem_spec, vmem_spec, pl.BlockSpec(memory_space=pl.ANY), vmem_spec],
         out_specs=vmem_spec,
         scratch_shapes=[
-            pltpu.VMEM(gathered.shape, F32),
-            pltpu.VMEM((gathered.shape[0],) * 2, F32),
+            pltpu.VMEM(noise.shape, F32),
+            pltpu.VMEM((members, members), F32),
             pltpu.SemaphoreType.DMA,
         ],
-    )(pieces, gathered, ensemble, noise, picks)
+    )(pieces, gathered, noise, picks)
 
 
 def per_device(operator, ensemble, noise, observations, variances, rows):
     obs, var = observations.reshape(128, 128), variances.reshape(128, 128)
     pieces, gathered, picks = exchange(operator, ensemble, obs, var, rows.reshape(1, -1))
-    return update(pieces, gathered, ensemble, noise, picks)
+    return update(pieces, gathered, noise, picks)
 
 
 def solution(mesh):

time: 44.5 us -> 43.1 us (0.969)
  Pallas kernels: 44.4 us -> 42.9 us
    pallas_call x1, Pallas kernels: 35.7 us -> 34.9 us  [exchange(): pl.pallas_call(exchange_kernel, name='exchange', out_shape=(pltpu.VMEM((8...]
    pallas_call x1, Pallas kernels: 8.67 us -> 8.05 us  [update(): pl.pallas_call(update_kernel, name='update', out_shape=jax.ShapeDtypeStru...]
where the time goes in v4:
time: 43.1 us; the launch traced here: 43 us
  Pallas kernels  42.9 us (100%)
    pallas_call x1, Pallas kernels, exchange(): pl.pallas_call(exchange_kernel, name='exchange', out_shape=(pltpu.VMEM((8...  34.9 us
    pallas_call x1, Pallas kernels, update(): pl.pallas_call(update_kernel, name='update', out_shape=jax.ShapeDtypeStru...  8.05 us

profile of v4, /device:TPU:1, one launch (start us, length us, event | category | flops | bytes accessed | tf_op | source)
XLA Modules:
  0.0 43.0 jit_solution(3004004704604843732)
XLA Ops:
  0.0 34.9 %exchange.1 = (f32[8,2,8,8,128]{4,3,2,1,0:T(8,128)S(1)}, f32[256,2048]{1,0:T(8,128)S(1)}, f32[8,512]{1,0:T(8,128)S(1)}) custom-call(f32[2048,512]{1,0:T(8,128)} %op_hbm.1, f32[32,2048]{1,0:T(8,128)} %ens_hbm.1, f32[128,128]{1,0:T(8,128)} %bitcast.3, f32[128,128]{1,0:T(8,128)} %bitcast.4, s32[1,512]{1,0:T(1,128)} %bitcast.5), custom_call_target="tpu_custom_call" | custom-call | tf_op jit(solution)/shard_map/exchange/pallas_call | solution.py:206
  34.9 8.0 %update.1 = f32[32,2048]{1,0:T(8,128)} custom-call(f32[8,2,8,8,128]{4,3,2,1,0:T(8,128)S(1)} %get-tuple-element.8.fwd_ref, f32[256,2048]{1,0:T(8,128)S(1)} %get-tuple-element.9.ens_ref, f32[32,512]{1,0:T(8,128)} %noise_hbm.1, f32[8,512]{1,0:T(8,128)S(1)} %get-tuple-element.10.picks_ref), custom_call_target="tpu_custom_call" | custom-call | tf_op jit(solution)/shard_map/update/pallas_call | solution.py:344

commit v5 on v4

--- a/solution.py
+++ b/solution.py
@@ -8,10 +8,20 @@
 MESH = pl.DeviceIdType.MESH
 CHUNKS = 4
 BLOCK = 32
+NEARX = 0
+EPOS = 1
+SPLIT = 0
 FRONTS = {0: (0, 16), 12: (16, 32)}
 FAR_FIRST = (4, 3, 5, 2, 6, 1, 7)
 NEAR = (1, 7, 2, 6)
 FAR = (4, 3, 5)
+
+
+def slot_of(d):
+    return jnp.where(d == 0, 0, jnp.where(d <= 4, 2 * d - 1, 2 * (8 - d)))
+
+
+SLOTS = (0, 1, 3, 5, 7, 6, 4, 2)
 F32 = jnp.float32
 BF16 = jnp.bfloat16
 
@@ -49,7 +59,7 @@
 def exchange_kernel(
     op_hbm, ens_hbm, obs_hbm, var_hbm, rows_hbm, fwd_all, ens_all, picks,
     op_v, obs_v, var_v, rows_v, source, came_one, middle, came_two,
-    op_sem, load_sem, send_sem, one_r, two_r, three_r, x_r, twin_r, ens_r, ens_twin_r,
+    op_sem, load_sem, send_sem, one_r, two_r, three_r, near_r, far_r, cross_r, twin_r, ens_r, ens_twin_r,
 ):
     mem = lax.axis_index("mem")
     par = lax.axis_index("par")
@@ -83,7 +93,7 @@
 
     barrier = pltpu.get_barrier_semaphore()
     friends = [at(d) for d in FAR_FIRST for at in across]
-    friends += [(mem_at(d), par) for d in (2, 1, 3)] + [(twin, par)]
+    friends += [(((x + d) % 4) * 2 + c, par) for d in (2, 1, 3) for c in range(2)] + [(twin, par)]
     for friend in friends:
         pl.semaphore_signal(barrier, inc=1, device_id=friend, device_id_type=MESH)
 
@@ -122,8 +132,22 @@
         for h in range(2):
             piece = source.at[h, (place[h] + d) % 8]
             copy_to(piece, came_one.at[h, d], send_sem.at[0], one_r.at[h], across[h](d)).start()
-    for d in (1, 3):
-        copy_to(own_ens, own_ens, send_sem.at[3], ens_r.at[d], (mem_at(d), par)).start()
+    half = own // 2
+    turns = ((0, 1), (1, 3))
+
+    def ens_rows(d, first, count):
+        return pl.ds(pl.multiple_of(((x + 4 - d) % 4) * 2 * own + core * own + first, count), count)
+
+    def ens_to_mem(lines, d, recv):
+        copy_to(ens_all.at[lines], ens_all.at[lines], send_sem.at[3], ens_r.at[recv], (mem_at(d), par)).start()
+
+    def ens_to_twin(lines):
+        copy_to(ens_all.at[lines], ens_all.at[lines], send_sem.at[4], ens_twin_r, (twin, par)).start()
+
+    for i, d in turns:
+        ens_to_mem(ens_rows(0, i * half, half), d, d)
+    for i, d in turns:
+        ens_to_mem(ens_rows(0, (1 - i) * half, half), d, 4 + i)
     copy_to(own_ens, own_ens, send_sem.at[4], ens_twin_r, (twin, par)).start()
 
     for copy in small:
@@ -141,60 +165,96 @@
         middle[h] = part[h]
         for d in FAR_FIRST:
             copy_to(middle.at[h], came_two.at[h, d], send_sem.at[1], two_r.at[h], along[h](d)).start()
+    def ens_onward():
+        for i, d in turns:
+            lines = ens_rows(d, i * half, half)
+            arrived(ens_all.at[lines], ens_r.at[d])
+            ens_to_mem(lines, d, 2 * i)
+            ens_to_twin(lines)
+
+    def ens_rest():
+        for i, d in turns:
+            lines = ens_rows(d, (1 - i) * half, half)
+            arrived(ens_all.at[lines], ens_r.at[4 + i])
+            ens_to_twin(lines)
+
+    if EPOS > 0:
+        ens_onward()
     for h in range(2):
         arrived(came_two.at[h, others], two_r.at[h])
         for d in range(1, 8):
             part[h] += came_two[h, d]
-        fwd_all[mem, h, place[h]] = part[h]
-        piece = fwd_all.at[mem, h, place[h]]
+        fwd_all[mem, h, 0] = part[h]
         for d in FAR_FIRST:
-            copy_to(piece, piece, send_sem.at[2], three_r.at[int(d in FAR), h], across[h](d)).start()
-
-    def spread_piece(h, d):
-        piece = fwd_all.at[mem, h, (place[h] + 8 - d) % 8]
-        for e in (2, 1, 3):
-            copy_to(piece, piece, send_sem.at[5], x_r.at[int(d in FAR)], (mem_at(e), par)).start()
-        copy_to(piece, piece, send_sem.at[6], twin_r, (twin, par)).start()
-
-    def ens_rows(d, first, count):
-        return pl.ds(pl.multiple_of(((x + 4 - d) % 4) * 2 * own + core * own + first, count), count)
-
-    def ens_to_twin(lines):
-        copy_to(ens_all.at[lines], ens_all.at[lines], send_sem.at[4], ens_twin_r, (twin, par)).start()
-
-    half = own // 2
+            copy_to(
+                fwd_all.at[mem, h, 0], fwd_all.at[mem, h, SLOTS[d]],
+                send_sem.at[2], three_r.at[int(d in FAR), h], across[h](d),
+            ).start()
+
+    near, far = pl.ds(0, 5), pl.ds(5, 3)
+
+    def mem_from(d):
+        return ((x + 4 - d) % 4) * 2 + core
+
+    def blocks(m, slots):
+        if SPLIT == 0:
+            return [fwd_all.at[m, :, slots]]
+        if SPLIT == 1:
+            return [fwd_all.at[m, h, slots] for h in range(2)]
+        return [fwd_all.at[m, h, i] for i in range(slots.start, slots.start + slots.size) for h in range(2)]
+
+    def to_mem(m, slots, d, send, recv):
+        for block in blocks(m, slots):
+            copy_to(block, block, send_sem.at[send], recv, (mem_at(d), par)).start()
+
+    def to_twin(m, slots):
+        for block in blocks(m, slots):
+            copy_to(block, block, send_sem.at[6], twin_r, (twin, par)).start()
+
+    def to_cross(m, slots, d, send, recv):
+        for block in blocks(m, slots):
+            copy_to(block, block, send_sem.at[send], recv, (((x + d) % 4) * 2 + 1 - core, par)).start()
+
+    if EPOS == 0:
+        ens_onward()
+    if EPOS != 2:
+        ens_rest()
     for h in range(2):
-        spread_piece(h, 0)
-    for i, d in ((0, 1), (1, 3)):
-        arrived(ens_all.at[ens_rows(d, 0, own)], ens_r.at[d])
-        lines = ens_rows(d, i * half, half)
-        copy_to(ens_all.at[lines], ens_all.at[lines], send_sem.at[3], ens_r.at[2 * i], (mem_at(d), par)).start()
-        ens_to_twin(ens_rows(d, 0, own))
-    for far, group in enumerate((NEAR, FAR)):
-        for h in range(2):
-            arrived(fwd_all.at[mem, h, pl.ds(0, len(group))], three_r.at[far, h])
-            for d in group:
-                spread_piece(h, d)
+        arrived(fwd_all.at[mem, h, pl.ds(0, 4)], three_r.at[0, h])
+    for d in (2, 1, 3):
+        to_mem(mem, near, d, 5, near_r.at[d - 1])
+        if NEARX:
+            to_cross(mem, near, d, 6, twin_r)
+    to_twin(mem, near)
+    for h in range(2):
+        arrived(fwd_all.at[mem, h, far], three_r.at[1, h])
+    for d in (2, 1, 3):
+        to_mem(mem, far, d, 7, far_r)
+        to_cross(mem, far, d, 7, cross_r)
+    block = fwd_all.at[mem, :, far]
+    copy_to(block, block, send_sem.at[7], cross_r, (twin, par)).start()
+    if EPOS == 2:
+        ens_rest()
+    for d in (1, 3, 2):
+        arrived(fwd_all.at[mem_from(d), :, near], near_r.at[d - 1])
+        if not NEARX:
+            to_twin(mem_from(d), near)
     for i in range(2):
         lines = ens_rows(2, i * half, half)
         arrived(ens_all.at[lines], ens_r.at[2 * i])
         ens_to_twin(lines)
-    for far, group in enumerate(((0,) + NEAR, FAR)):
-        arrived(fwd_all.at[pl.ds(0, 3), :, pl.ds(0, len(group))], x_r.at[far])
-        for d in group:
-            for h in range(2):
-                for e in (1, 3, 2):
-                    piece = fwd_all.at[((x + 4 - e) % 4) * 2 + core, h, (place[h] + 8 - d) % 8]
-                    copy_to(piece, piece, send_sem.at[6], twin_r, (twin, par)).start()
-    arrived(fwd_all.at[pl.ds(0, 4)], twin_r)
+    arrived(fwd_all.at[pl.ds(0, 3), :, far], far_r)
+    arrived(fwd_all.at[pl.ds(0, 4), :, far], cross_r)
+    arrived(fwd_all.at[pl.ds(0, 4), :, near], twin_r)
     arrived(ens_all.at[pl.ds(0, 4 * own)], ens_twin_r)
     for i in range(2):
         sent(came_one.at[:, others], send_sem.at[i])
     sent(came_one.at[:, others], send_sem.at[2])
     sent(ens_all.at[pl.ds(0, 3 * own)], send_sem.at[3])
     sent(ens_all.at[pl.ds(0, 4 * own)], send_sem.at[4])
-    sent(fwd_all.at[pl.ds(0, 3)], send_sem.at[5])
-    sent(fwd_all.at[pl.ds(0, 4)], send_sem.at[6])
+    sent(fwd_all.at[pl.ds(0, 3), :, near], send_sem.at[5])
+    sent(fwd_all.at[pl.ds(0, 7), :, far], send_sem.at[7])
+    sent(fwd_all.at[pl.ds(0, 4), :, near], send_sem.at[6])
 
 
 def exchange(operator, ensemble, obs, var, rows):
@@ -222,8 +282,8 @@
             pltpu.VMEM((2, 8, 8, 128), F32),
             pltpu.VMEM((2, 8, 128), F32),
             pltpu.VMEM((2, 8, 8, 128), F32),
-            dma((CHUNKS,)), dma((4,)), dma((7,)),
-            dma((2,)), dma((2,)), dma((2, 2)), dma((2,)), dma, dma((4,)), dma,
+            dma((CHUNKS,)), dma((4,)), dma((8,)),
+            dma((2,)), dma((2,)), dma((2, 2)), dma((3,)), dma, dma, dma, dma((6,)), dma,
         ],
         compiler_params=pltpu.CompilerParams(collective_id=0, has_side_effects=True),
     )(operator, ensemble, obs, var, rows)
@@ -301,14 +361,17 @@
     return product(a_hi, b_hi) + product(a_lo, b_hi) + product(a_hi, b_lo)
 
 
-def update_kernel(fwd_ref, ens_ref, noise_hbm, picks_ref, out_ref, noise_v, m_ref, noise_sem):
+def update_kernel(fwd_ref, ens_ref, noise_hbm, picks_ref, out_hbm, noise_v, m_ref, out_v, noise_sem, out_sem):
     mem = lax.axis_index("mem")
-    own = out_ref.shape[0]
+    own = out_hbm.shape[0]
     noise_copy = pltpu.make_async_copy(noise_hbm, noise_v, noise_sem)
     noise_copy.start()
 
+    par = lax.axis_index("par")
+    slots = [[slot_of((at + 8 - q) % 8) for q in range(8)] for at in (par % 8, par // 8)]
+
     def rows_of(m):
-        lines = [[fwd_ref[m, h, r * 2 + l] for h in range(2) for l in range(2)] for r in range(4)]
+        lines = [[fwd_ref[m, h, slots[h][r * 2 + l]] for h in range(2) for l in range(2)] for r in range(4)]
         return jnp.concatenate([jnp.concatenate(line, axis=1) for line in lines], axis=0)
 
     forward = jnp.concatenate([rows_of(m) for m in range(8)], axis=0)
@@ -329,9 +392,14 @@
     weights = weights - jnp.mean(weights, axis=1, keepdims=True)
     own_rows = pl.ds(pl.multiple_of(mem * own, own), own)
     step = 512
-    for c in range(out_ref.shape[1] // step):
+    copies = []
+    for c in range(out_hbm.shape[1] // step):
         part = pl.ds(c * step, step)
-        out_ref[:, part] = ens_ref[own_rows, part] + dot3(weights, ens_ref[:, part])
+        out_v[:, part] = ens_ref[own_rows, part] + dot3(weights, ens_ref[:, part])
+        copies.append(pltpu.make_async_copy(out_v.at[:, part], out_hbm.at[:, part], out_sem.at[c]))
+        copies[-1].start()
+    for copy in copies:
+        copy.wait()
 
 
 def update(pieces, gathered, noise, picks):
@@ -346,11 +414,13 @@
         name="update",
         out_shape=jax.ShapeDtypeStruct((own, params), F32),
         in_specs=[vmem_spec, vmem_spec, pl.BlockSpec(memory_space=pl.ANY), vmem_spec],
-        out_specs=vmem_spec,
+        out_specs=pl.BlockSpec(memory_space=pl.ANY),
         scratch_shapes=[
             pltpu.VMEM(noise.shape, F32),
             pltpu.VMEM((members, members), F32),
+            pltpu.VMEM((own, params), F32),
             pltpu.SemaphoreType.DMA,
+            pltpu.SemaphoreType.DMA((4,)),
         ],
     )(pieces, gathered, noise, picks)
 

time: 43.1 us -> 43 us (level)
  no operation moved by 1% of the time
where the time goes in v5:
time: 43 us; the launch traced here: 42.9 us
  Pallas kernels  42.9 us (100%)
    pallas_call x1, Pallas kernels, exchange(): pl.pallas_call(exchange_kernel, name='exchange', out_shape=(pltpu.VMEM((8...  34.8 us
    pallas_call x1, Pallas kernels, update(): pl.pallas_call(update_kernel, name='update', out_shape=jax.ShapeDtypeStru...  8.08 us

profile of v5, /device:TPU:1, one launch (start us, length us, event | category | flops | bytes accessed | tf_op | source)
XLA Modules:
  0.0 42.9 jit_solution(228380534367453913)
XLA Ops:
  0.0 34.8 %exchange.1 = (f32[8,2,8,8,128]{4,3,2,1,0:T(8,128)S(1)}, f32[256,2048]{1,0:T(8,128)S(1)}, f32[8,512]{1,0:T(8,128)S(1)}) custom-call(f32[2048,512]{1,0:T(8,128)} %op_hbm.1, f32[32,2048]{1,0:T(8,128)} %ens_hbm.1, f32[128,128]{1,0:T(8,128)} %bitcast.3, f32[128,128]{1,0:T(8,128)} %bitcast.4, s32[1,512]{1,0:T(1,128)} %bitcast.5), custom_call_target="tpu_custom_call" | custom-call | tf_op jit(solution)/shard_map/exchange/pallas_call | solution.py:266
  34.8 8.1 %update.1 = f32[32,2048]{1,0:T(8,128)} custom-call(f32[8,2,8,8,128]{4,3,2,1,0:T(8,128)S(1)} %get-tuple-element.8.fwd_ref, f32[256,2048]{1,0:T(8,128)S(1)} %get-tuple-element.9.ens_ref, f32[32,512]{1,0:T(8,128)} %noise_hbm.1, f32[8,512]{1,0:T(8,128)S(1)} %get-tuple-element.10.picks_ref), custom_call_target="tpu_custom_call" | custom-call | tf_op jit(solution)/shard_map/update/pallas_call | solution.py:412
